TPU v7x, 32 devices: a whole 2x2x4 slice. The times are simulated.
32 devices in a mesh: dp: 8 (over z, y), mp: 4 (over x, core).
Axes of the slice: x: 2, y: 2, z: 4, core: 2. Of those that a mesh axis runs over, the one named last changes fastest.
Arguments:
- block_in: bfloat16 [16384, 1536], P('dp'), may hold values from -6 to 6
- cotangent: bfloat16 [16384, 1536], P('dp'), may hold values from -6 to 6
- segment_ids: int32 [32, 512], P('dp'), may hold values from 0 to 2, never falling along the last dimension, each value on 1 to 256 neighbouring positions
- w_heads: float32 [3, 1536, 3072], P(None, 'dp', 'mp'), may hold values from -0.15625 to 0.15625
- w_bc: float32 [1536, 256], P('dp', 'mp'), may hold values from -0.15625 to 0.15625
- w_dt: float32 [1536, 48], P('dp', 'mp'), may hold values from -0.15625 to 0.15625
- mom_heads: float32 [3, 1536, 3072], P(None, 'dp', 'mp'), may hold values from -160 to 160
- mom_bc: float32 [1536, 256], P('dp', 'mp'), may hold values from -160 to 160
- mom_dt: float32 [1536, 48], P('dp', 'mp'), may hold values from -160 to 160
- norm_gain: float32 [1536], replicated, may hold values from 0.5 to 1.5
- inner_params: float32 [6, 3072], P(None, 'mp'), may hold values from -0.6 to 1
- bc_params: float32 [5, 256], P(None, 'mp'), may hold values from -0.6 to 1
- head_params: float32 [3, 48], P(None, 'mp'), may hold values from -5 to 4.5
- norm_adam: float32 [2, 1536], replicated, may hold values from -11.52 to 11.52, as said below
- inner_adam: float32 [2, 6, 3072], P(None, None, 'mp'), may hold values from -11.52 to 11.52, as said below
- bc_adam: float32 [2, 5, 256], P(None, None, 'mp'), may hold values from -11.52 to 11.52, as said below
- head_adam: float32 [2, 3, 48], P(None, None, 'mp'), may hold values from -11.52 to 11.52, as said below
Outputs:
- block_out: bfloat16 [16384, 1536], P('dp')
- grad_block: float32 [16384, 1536], P('dp')
- grad_heads: float32 [3, 1536, 3072], P(None, 'dp', 'mp')
- grad_bc: float32 [1536, 256], P('dp', 'mp')
- grad_dt: float32 [1536, 48], P('dp', 'mp')
- grad_norm_gain: float32 [1536], replicated
- grad_inner: float32 [6, 3072], P(None, 'mp')
- grad_bc_params: float32 [5, 256], P(None, 'mp')
- grad_head_params: float32 [3, 48], P(None, 'mp')
- new_w_heads: float32 [3, 1536, 3072], P(None, 'dp', 'mp')
- new_w_bc: float32 [1536, 256], P('dp', 'mp')
- new_w_dt: float32 [1536, 48], P('dp', 'mp')
- new_mom_heads: float32 [3, 1536, 3072], P(None, 'dp', 'mp')
- new_mom_bc: float32 [1536, 256], P('dp', 'mp')
- new_mom_dt: float32 [1536, 48], P('dp', 'mp')
- new_norm_gain: float32 [1536], replicated
- new_inner_params: float32 [6, 3072], P(None, 'mp')
- new_bc_params: float32 [5, 256], P(None, 'mp')
- new_head_params: float32 [3, 48], P(None, 'mp')
- new_norm_adam: float32 [2, 1536], replicated
- new_inner_adam: float32 [2, 6, 3072], P(None, None, 'mp')
- new_bc_adam: float32 [2, 5, 256], P(None, None, 'mp')
- new_head_adam: float32 [2, 3, 48], P(None, None, 'mp')
Inputs may be any that keep to these rules, and one draw needn't show every extreme that they name: `segment_ids`: segment numbers of one sequence never fall; a document holds at most 256 tokens. `norm_adam`: row 0 holds first moments, row 1 second moments, which are positive. `inner_adam`: row 0 holds first moments, row 1 second moments, which are positive. `bc_adam`: row 0 holds first moments, row 1 second moments, which are positive. `head_adam`: row 0 holds first moments, row 1 second moments, which are positive.
All inputs are finite; a program needn't handle non-finite values.
Results may differ from a plain program's by a relative error of at most 0.0017.
The roundings to bfloat16 on the way count: a program that leaves them out, or rounds other values in their place, can miss the bound.
Values may be sent and summed in bfloat16 or wider, within the bound.
No kernel may reach another device: no remote copies, remote signals or barrier semaphores. Data moves between devices by JAX's collectives and lax.ppermute only.
A program may use at most 256 MiB of HBM per device.

v0:
```python
import math

import jax
import jax.numpy as jnp
from jax import lax
from jax.sharding import PartitionSpec as P

D = 1536
HEADS = 48
HEADDIM = 64
STATE = 128
CONV = 4
SPAN = 256
NS_STEPS = 5
INNER = 3072


highest = lax.Precision.HIGHEST
eps_norm = 1e-05
ns_coeffs = (3.4445, -4.775, 2.0315)
momentum_beta = 0.95
muon_rate = 0.02
decay_rate = 0.1
adam_rate = 0.1
adam_first = 0.9
adam_second = 0.999
adam_steps = 2.0


def causal_conv(values, conv_par, segments):
    result = conv_par[CONV] + conv_par[CONV - 1] * values
    for offset in range(1, CONV):
        shifted = jnp.pad(values[:, :-offset], ((0, 0), (offset, 0), (0, 0)))
        earlier = jnp.pad(segments[:, :-offset], ((0, 0), (offset, 0)), constant_values=-1)
        linked = (earlier == segments)[:, :, None]
        result = result + conv_par[CONV - 1 - offset] * jnp.where(linked, shifted, 0.0)
    return result


def convolve_state(raw_vals, conv_par, segments):
    return jax.nn.silu(causal_conv(raw_vals, conv_par, segments))


def mixer(x_raw, gate_z, step_raw, state_vals, conv_par, head_par, segments):
    x_conv = jax.nn.silu(causal_conv(x_raw[None], conv_par, segments[None])[0])
    length = x_raw.shape[0]
    head_count = step_raw.shape[1]
    head_width = x_raw.shape[1] // head_count
    state_size = state_vals.shape[1] // 2
    blocks = length // SPAN
    step_size = jax.nn.softplus(step_raw + head_par[1])
    log_decay = -jnp.exp(head_par[0]) * step_size
    x_heads = x_conv.reshape(blocks, SPAN, head_count, head_width)
    inputs = x_heads * step_size.reshape(blocks, SPAN, head_count, 1)
    b_mat = state_vals[:, :state_size].reshape(blocks, SPAN, state_size)
    c_mat = state_vals[:, state_size:].reshape(blocks, SPAN, state_size)
    seg_blocks = segments.reshape(blocks, SPAN)
    cumul = jnp.cumsum(log_decay.reshape(blocks, SPAN, head_count), axis=1)
    cum_heads = jnp.swapaxes(cumul, 1, 2)
    scores = jnp.einsum("ctn,csn->cts", c_mat, b_mat, precision=highest)
    positions = jnp.arange(SPAN)
    allowed = (positions[:, None] >= positions[None, :]) & (
        seg_blocks[:, :, None] == seg_blocks[:, None, :]
    )
    gaps = cum_heads[:, :, :, None] - cum_heads[:, :, None, :]
    weights = jnp.exp(jnp.where(allowed[:, None], gaps, -jnp.inf)) * scores[:, None]
    inner_out = jnp.einsum("chts,cshp->cthp", weights, inputs, precision=highest)
    span_total = cumul[:, SPAN - 1, :]
    tail_ok = seg_blocks == seg_blocks[:, SPAN - 1 :]
    tail_decay = jnp.exp(jnp.where(tail_ok[:, :, None], span_total[:, None, :] - cumul, -jnp.inf))
    states = jnp.einsum("cshp,csn->chpn", inputs * tail_decay[..., None], b_mat, precision=highest)
    carried = jnp.zeros((head_count, head_width, state_size), jnp.float32)
    prev_end = jnp.full((), -1, segments.dtype)
    carried_out = []
    for block_idx in range(blocks):
        entry_ok = seg_blocks[block_idx] == prev_end
        head_decay = jnp.exp(cumul[block_idx])
        contrib = (
            jnp.einsum("tn,hpn->thp", c_mat[block_idx], carried, precision=highest)
            * head_decay[:, :, None]
        )
        carried_out.append(jnp.where(entry_ok[:, None, None], contrib, 0.0))
        keep_state = seg_blocks[block_idx, SPAN - 1] == prev_end
        carried = (
            jnp.where(keep_state, jnp.exp(span_total[block_idx])[:, None, None] * carried, 0.0)
            + states[block_idx]
        )
        prev_end = seg_blocks[block_idx, SPAN - 1]
    mixed_heads = inner_out + jnp.stack(carried_out) + head_par[2][:, None] * x_heads
    return mixed_heads.reshape(length, head_count * head_width) * jax.nn.silu(gate_z)


def run_mixer(x_raw, gate_z, step_raw, state_vals, conv_par, head_par, segments):
    seq_here, length = segments.shape

    def per_sequence(item):
        return mixer(item[0], item[1], item[2], item[3], conv_par, head_par, item[4])

    stacked = lax.map(
        per_sequence,
        (
            x_raw.reshape(seq_here, length, -1),
            gate_z.reshape(seq_here, length, -1),
            step_raw.reshape(seq_here, length, -1),
            state_vals.reshape(seq_here, length, -1),
            segments,
        ),
    )
    return stacked.reshape(seq_here * length, -1)


def run_mixer_back(x_raw, gate_z, step_raw, state_vals, conv_par, head_par, segments, d_mixed):
    seq_here, length = segments.shape

    def per_sequence(item):

        def local_fn(a, b, c, d, e, f):
            return mixer(a, b, c, d, e, f, item[4])

        primal, back_fn = jax.vjp(local_fn, item[0], item[1], item[2], item[3], conv_par, head_par)
        return back_fn(item[5])

    grads = lax.map(
        per_sequence,
        (
            x_raw.reshape(seq_here, length, -1),
            gate_z.reshape(seq_here, length, -1),
            step_raw.reshape(seq_here, length, -1),
            state_vals.reshape(seq_here, length, -1),
            segments,
            d_mixed.reshape(seq_here, length, -1),
        ),
    )
    tok_rows = seq_here * length
    return (
        grads[0].reshape(tok_rows, -1),
        grads[1].reshape(tok_rows, -1),
        grads[2].reshape(tok_rows, -1),
        grads[3].reshape(tok_rows, -1),
        jnp.sum(grads[4], axis=0),
        jnp.sum(grads[5], axis=0),
    )


def gated_norm(mixed, squares, gain_row):
    return mixed * lax.rsqrt(squares / INNER + eps_norm)[:, None] * gain_row


def input_norm(features, gain_row):
    return (
        features
        * lax.rsqrt(jnp.mean(features * features, axis=1, keepdims=True) + eps_norm)
        * gain_row
    )


def orthogonalize(blocks_in):
    frob_norm = jnp.sqrt(jnp.sum(blocks_in * blocks_in, axis=(1, 2), keepdims=True))
    current = blocks_in / (frob_norm + 1e-07)
    for sweep_idx in range(NS_STEPS):
        gram_mat = jnp.einsum("kdp,kdq->kpq", current, current, precision=highest)
        poly_mat = ns_coeffs[1] * gram_mat + ns_coeffs[2] * jnp.einsum(
            "kpq,kqr->kpr", gram_mat, gram_mat, precision=highest
        )
        current = ns_coeffs[0] * current + jnp.einsum(
            "kdp,kpq->kdq", current, poly_mat, precision=highest
        )
    return current


def orth_items(received):
    item_count = received.shape[0]
    return orthogonalize(received.reshape(item_count, -1, HEADDIM)).reshape(received.shape)


def adam_update(params_in, gradient, state_pair):
    moment_one = adam_first * state_pair[0] + (1.0 - adam_first) * gradient
    moment_two = adam_second * state_pair[1] + (1.0 - adam_second) * gradient * gradient
    scaled = (
        moment_one
        / (1.0 - adam_first**adam_steps)
        / (jnp.sqrt(moment_two / (1.0 - adam_second**adam_steps)) + 1e-08)
    )
    return (params_in - adam_rate * scaled, jnp.stack([moment_one, moment_two]))


def muon_update(weight_vals, ortho_vals):
    return weight_vals - muon_rate * (0.2 * math.sqrt(D) * ortho_vals + decay_rate * weight_vals)


def body(
    block_in,
    cotangent,
    segment_ids,
    w_heads,
    w_bc,
    w_dt,
    mom_heads,
    mom_bc,
    mom_dt,
    norm_gain,
    inner_params,
    bc_params,
    head_params,
    norm_adam,
    inner_adam,
    bc_adam,
    head_adam,
):
    seq_here, length = segment_ids.shape
    tok_rows = seq_here * length
    gathered = (
        lax.all_gather(w_heads.astype(jnp.bfloat16), "dp", axis=1, tiled=True),
        lax.all_gather(w_bc.astype(jnp.bfloat16), "dp", axis=0, tiled=True),
        lax.all_gather(w_dt.astype(jnp.bfloat16), "dp", axis=0, tiled=True),
    )
    w_zed = gathered[0][0]
    w_xin = gathered[0][1]
    w_out = gathered[0][2]
    w_state = gathered[1]
    w_step = gathered[2]
    x_float = block_in.astype(jnp.float32)
    normed = input_norm(x_float, norm_gain).astype(jnp.bfloat16)
    gate_z = jnp.dot(normed, w_zed, preferred_element_type=jnp.float32)
    x_raw = jnp.dot(normed, w_xin, preferred_element_type=jnp.float32)
    state_raw = jnp.dot(normed, w_state, preferred_element_type=jnp.float32).reshape(
        seq_here, length, -1
    )
    step_raw = jnp.dot(normed, w_step, preferred_element_type=jnp.float32)
    state_own = (
        convolve_state(state_raw, bc_params, segment_ids).reshape(tok_rows, -1).astype(jnp.bfloat16)
    )
    state_vals = lax.all_gather(state_own, "mp", axis=1, tiled=True).astype(jnp.float32)
    conv_inner = inner_params[: CONV + 1]
    gate_gain = inner_params[CONV + 1]
    mixed = run_mixer(x_raw, gate_z, step_raw, state_vals, conv_inner, head_params, segment_ids)
    squares = lax.psum(jnp.sum(mixed * mixed, axis=1), "mp")
    out_bf = gated_norm(mixed, squares, gate_gain).astype(jnp.bfloat16)
    branch_part = jnp.einsum("rc,dc->rd", out_bf, w_out, preferred_element_type=jnp.float32)
    branch_sum = lax.psum(branch_part, "mp")
    block_out = (x_float + branch_sum).astype(jnp.bfloat16)
    back_out = jnp.einsum("rd,dc->rc", cotangent, w_out, preferred_element_type=jnp.float32)
    grad_wout = jnp.einsum("rd,rc->dc", cotangent, out_bf, preferred_element_type=jnp.float32)
    primal, gate_back = jax.vjp(gated_norm, mixed, squares, gate_gain)
    back_mixed, back_squares, back_gain = gate_back(back_out)
    back_squares = lax.psum(back_squares, "mp")
    back_mixed = back_mixed + 2.0 * mixed * back_squares[:, None]
    back_xraw, back_gate, back_step, back_state, back_conv, back_head = run_mixer_back(
        x_raw, gate_z, step_raw, state_vals, conv_inner, head_params, segment_ids, back_mixed
    )
    state_share = lax.psum_scatter(back_state, "mp", scatter_dimension=1, tiled=True)

    def state_fn(raw_vals, conv_par):
        return convolve_state(raw_vals, conv_par, segment_ids)

    primal, state_back = jax.vjp(state_fn, state_raw, bc_params)
    back_sraw, back_bcpar = state_back(state_share.reshape(seq_here, length, -1))
    gate_bf = back_gate.astype(jnp.bfloat16)
    xraw_bf = back_xraw.astype(jnp.bfloat16)
    sraw_bf = back_sraw.reshape(tok_rows, -1).astype(jnp.bfloat16)
    step_bf = back_step.astype(jnp.bfloat16)
    back_normed = jnp.einsum("rc,dc->rd", gate_bf, w_zed, preferred_element_type=jnp.float32)
    back_normed = back_normed + jnp.einsum(
        "rc,dc->rd", xraw_bf, w_xin, preferred_element_type=jnp.float32
    )
    back_normed = back_normed + jnp.einsum(
        "rc,dc->rd", sraw_bf, w_state, preferred_element_type=jnp.float32
    )
    back_normed = back_normed + jnp.einsum(
        "rc,dc->rd", step_bf, w_step, preferred_element_type=jnp.float32
    )
    grad_zed = jnp.einsum("rd,rc->dc", normed, gate_bf, preferred_element_type=jnp.float32)
    grad_xin = jnp.einsum("rd,rc->dc", normed, xraw_bf, preferred_element_type=jnp.float32)
    grad_state = jnp.einsum("rd,rc->dc", normed, sraw_bf, preferred_element_type=jnp.float32)
    grad_step = jnp.einsum("rd,rc->dc", normed, step_bf, preferred_element_type=jnp.float32)
    normed_sum = lax.psum(back_normed, "mp")
    primal, norm_back = jax.vjp(input_norm, x_float, norm_gain)
    back_x, back_ngain = norm_back(normed_sum)
    grad_block = cotangent.astype(jnp.float32) + back_x
    grad_parts = (
        lax.psum_scatter(
            jnp.stack([grad_zed, grad_xin, grad_wout]), "dp", scatter_dimension=1, tiled=True
        ),
        lax.psum_scatter(grad_state, "dp", scatter_dimension=0, tiled=True),
        lax.psum_scatter(grad_step, "dp", scatter_dimension=0, tiled=True),
    )
    grad_heads = grad_parts[0]
    grad_bc = grad_parts[1]
    grad_dt = grad_parts[2]
    vector_sums = lax.psum(
        (back_ngain, jnp.concatenate([back_conv, back_gain[None]], axis=0), back_bcpar, back_head),
        "dp",
    )
    grad_norm_gain = vector_sums[0]
    grad_inner = vector_sums[1]
    grad_bc_params = vector_sums[2]
    grad_head_params = vector_sums[3]
    new_mom_heads = momentum_beta * mom_heads + grad_heads
    new_mom_bc = momentum_beta * mom_bc + grad_bc
    new_mom_dt = momentum_beta * mom_dt + grad_dt
    rows_here = w_heads.shape[1]
    cols_here = w_heads.shape[2]
    heads_here = cols_here // HEADDIM
    state_cols = w_bc.shape[1]
    steps_here = w_dt.shape[1]
    matrices = (
        new_mom_heads.reshape(3, rows_here, heads_here, HEADDIM)
        .transpose(0, 2, 1, 3)
        .reshape(3 * heads_here, rows_here, HEADDIM)
    )
    mats_here = matrices.shape[0]
    owner_count = lax.axis_size("dp")
    slot_count = (mats_here + owner_count - 1) // owner_count
    send_buffer = jnp.pad(
        matrices, ((0, slot_count * owner_count - mats_here), (0, 0), (0, 0))
    ).reshape(slot_count, owner_count, rows_here, HEADDIM)
    ortho_owned = orth_items(
        lax.all_to_all(send_buffer, "dp", split_axis=1, concat_axis=2, tiled=True)
    )
    returned = lax.all_to_all(ortho_owned, "dp", split_axis=2, concat_axis=1, tiled=True)
    ortho_flat = returned.reshape(slot_count * owner_count, rows_here, HEADDIM)[:mats_here]
    ortho_heads = (
        ortho_flat.reshape(3, heads_here, rows_here, HEADDIM)
        .transpose(0, 2, 1, 3)
        .reshape(3, rows_here, cols_here)
    )
    full_cols = (
        lax.all_gather(new_mom_bc, "mp", axis=1, tiled=True),
        lax.all_gather(new_mom_dt, "mp", axis=1, tiled=True),
    )
    full_bc = full_cols[0]
    full_dt = full_cols[1]
    current = jnp.stack(
        [full_bc[:, :STATE], full_bc[:, STATE:], jnp.pad(full_dt, ((0, 0), (0, STATE - HEADS)))]
    )
    for sweep_idx in range(NS_STEPS):
        gram_mat = lax.psum(jnp.einsum("kdp,kdq->kpq", current, current, precision=highest), "dp")
        if sweep_idx == 0:
            frob_norm = jnp.sqrt(jnp.sum(jnp.diagonal(gram_mat, axis1=1, axis2=2), axis=1))
            scale_now = (1.0 / (frob_norm + 1e-07))[:, None, None]
            current = current * scale_now
            gram_mat = gram_mat * (scale_now * scale_now)
        poly_mat = ns_coeffs[1] * gram_mat + ns_coeffs[2] * jnp.einsum(
            "kpq,kqr->kpr", gram_mat, gram_mat, precision=highest
        )
        current = ns_coeffs[0] * current + jnp.einsum(
            "kdp,kpq->kdq", current, poly_mat, precision=highest
        )
    mp_place = lax.axis_index("mp")
    ortho_bc_full = jnp.concatenate([current[0], current[1]], axis=1)
    ortho_state = lax.dynamic_slice_in_dim(ortho_bc_full, mp_place * state_cols, state_cols, 1)
    ortho_step = lax.dynamic_slice_in_dim(current[2], mp_place * steps_here, steps_here, 1)
    new_w_heads = muon_update(w_heads, ortho_heads)
    new_w_bc = muon_update(w_bc, ortho_state)
    new_w_dt = muon_update(w_dt, ortho_step)
    new_norm_gain, new_norm_adam = adam_update(norm_gain, grad_norm_gain, norm_adam)
    new_inner_params, new_inner_adam = adam_update(inner_params, grad_inner, inner_adam)
    new_bc_params, new_bc_adam = adam_update(bc_params, grad_bc_params, bc_adam)
    new_head_params, new_head_adam = adam_update(head_params, grad_head_params, head_adam)
    return (
        block_out,
        grad_block,
        grad_heads,
        grad_bc,
        grad_dt,
        grad_norm_gain,
        grad_inner,
        grad_bc_params,
        grad_head_params,
        new_w_heads,
        new_w_bc,
        new_w_dt,
        new_mom_heads,
        new_mom_bc,
        new_mom_dt,
        new_norm_gain,
        new_inner_params,
        new_bc_params,
        new_head_params,
        new_norm_adam,
        new_inner_adam,
        new_bc_adam,
        new_head_adam,
    )


def solution(mesh):
    in_specs = (
        P("dp", None),
        P("dp", None),
        P("dp", None),
        P(None, "dp", "mp"),
        P("dp", "mp"),
        P("dp", "mp"),
        P(None, "dp", "mp"),
        P("dp", "mp"),
        P("dp", "mp"),
        P(),
        P(None, "mp"),
        P(None, "mp"),
        P(None, "mp"),
        P(),
        P(None, None, "mp"),
        P(None, None, "mp"),
        P(None, None, "mp"),
    )
    out_specs = (
        P("dp", None),
        P("dp", None),
        P(None, "dp", "mp"),
        P("dp", "mp"),
        P("dp", "mp"),
        P(),
        P(None, "mp"),
        P(None, "mp"),
        P(None, "mp"),
        P(None, "dp", "mp"),
        P("dp", "mp"),
        P("dp", "mp"),
        P(None, "dp", "mp"),
        P("dp", "mp"),
        P("dp", "mp"),
        P(),
        P(None, "mp"),
        P(None, "mp"),
        P(None, "mp"),
        P(),
        P(None, None, "mp"),
        P(None, None, "mp"),
        P(None, None, "mp"),
    )
    return jax.shard_map(body, mesh=mesh, in_specs=in_specs, out_specs=out_specs, check_vma=False)
```

profile of v0, /device:TPU:0, one launch (start us, length us, event | category | flops | bytes accessed | tf_op | source)
XLA Modules:
  0.0 2318.2 jit_solution(16401024607752423164)
XLA Ops:
  12.3 32.6 %all-gather.1 = bf16[8,192,64]{1,2,0:T(8,128)(2,1)S(1)} all-gather(bf16[1,192,64]{1,2,0:T(8,128)(2,1)S(1)} %convert_bitcast_fusion), channel_id=1, replica_groups=mesh['dp'=8,'mp'=4] {'dp'}, dimensions={0}, use_global_device_ids=true | all-gather | bytes 221184 | tf_op jit(solution)/shard_map/all_gather | solution.py:214
  59.1 30.8 %all-gather = bf16[8,192,12]{1,2,0:T(8,128)(2,1)S(1)} all-gather(bf16[1,192,12]{1,2,0:T(8,128)(2,1)S(1)} %convert_bitcast_fusion.1), channel_id=1, replica_groups=mesh['dp'=8,'mp'=4] {'dp'}, dimensions={0}, use_global_device_ids=true | all-gather | bytes 41472 | tf_op jit(solution)/shard_map/all_gather | solution.py:215
  100.0 86.8 %all-gather.6.cloned.1.call-done = bf16[3,1536,768]{2,1,0:T(8,128)(2,1)} async-done(((bf16[3,192,768]{2,1,0:T(8,128)(2,1)}), bf16[3,1536,768]{2,1,0:T(8,128)(2,1)}) %all-gather.6.cloned.1.call-update) | async-done | bytes 7077904 | tf_op jit(solution)/shard_map/all_gather | solution.py:213
  186.7 9.9 fusion.155
  196.6 8.7 fusion.159
  205.3 148.1 %while.35 = (s32[]{:T(128)}, f32[4,512,768]{1,2,0:T(8,128)}, f32[5,768]{1,0:T(8,128)}, f32[4,512,768]{1,2,0:T(8,128)}, s32[4,512]{1,0:T(4,128)S(1)}, /*index=5*/...) while((s32[]{:T(128)}, f32[4,512,768]{1,2,0:T(8,128)}, ...), condition=%wide.region_4.5_spmd, body=%wide.region_1.4_spmd.sunk | while | flops 2335799808 | bytes 79394152 | solution.py:99
  369.3 11.5 multiply_reduce_fusion.12
  395.2 504.8 %while.36 = (s32[]{:T(128)}, bf16[4,512,768]{2,1,0:T(8,128)(2,1)}, bf16[4,512,768]{2,1,0:T(8,128)(2,1)}, bf16[4,512,12]{1,2,0:T(8,128)(2,1)}, f32[4,512,256]{2,1...) while((s32[]{:T(128)}, bf16[4,512,768]{2,1,0:T(8,128)(2,1)}, ...), condition=%wide.region_33.34_spmd, body=%wide.region_10.33_spmd.sunk | while | flops 7328152064 | bytes 223389664 | solution.py:123
  437.5 12.4 fusion.434
  561.6 12.7 fusion.434
  686.0 12.4 fusion.434
  810.2 12.7 fusion.434
  910.5 21.6 reduce-scatter.13.cloned.1.call-done
  945.9 53.2 %reduce-scatter.17.cloned.1.call-done = f32[192,12]{1,0:T(8,128)} async-done(((f32[1536,12]{1,0:T(8,128)}), f32[192,12]{1,0:T(8,128)}) %reduce-scatter.17.cloned.1.call-update) | async-done | bytes 9232
  1007.9 57.2 %reduce-scatter.15.cloned.1.call-done = f32[192,64]{1,0:T(8,128)} async-done(((f32[1536,64]{1,0:T(8,128)}), f32[192,64]{1,0:T(8,128)}) %reduce-scatter.15.cloned.1.call-update) | async-done | bytes 49168
  1075.4 9.2 convolution_bitcast_fusion.2
  1084.5 60.6 %all-reduce.57.cloned.1.call-done = f32[3,128,128]{2,1,0:T(8,128)} async-done(((f32[3,128,128]{2,1,0:T(8,128)}), f32[3,128,128]{2,1,0:T(8,128)}) %all-reduce.57.cloned.1.call-update) | async-done | bytes 196624 | tf_op jit(solution)/shard_map/psum | solution.py:337
  1155.0 9.6 convolution_bitcast_fusion.3
  1164.6 60.2 %all-reduce.59.cloned.1.call-done = f32[3,128,128]{2,1,0:T(8,128)} async-done(((f32[3,128,128]{2,1,0:T(8,128)}), f32[3,128,128]{2,1,0:T(8,128)}) %all-reduce.59.cloned.1.call-update) | async-done | bytes 196624 | tf_op jit(solution)/shard_map/psum | solution.py:337
  1228.1 9.6 convolution_bitcast_fusion.4
  1237.7 60.7 %all-reduce.61.cloned.1.call-done = f32[3,128,128]{2,1,0:T(8,128)} async-done(((f32[3,128,128]{2,1,0:T(8,128)}), f32[3,128,128]{2,1,0:T(8,128)}) %all-reduce.61.cloned.1.call-update) | async-done | bytes 196624 | tf_op jit(solution)/shard_map/psum | solution.py:337
  1301.7 11.1 pad_maximum_fusion
  1317.2 10.1 fusion.157
  1350.2 21.8 all-reduce.63.cloned.1.call-done
  1375.3 18.6 add_add_fusion.1
  1397.6 207.3 %reduce-scatter.11.cloned.1.call-done = f32[3,192,768]{2,1,0:T(8,128)} async-done(((f32[3,1536,768]{2,1,0:T(8,128)}), f32[3,192,768]{2,1,0:T(8,128)}) %reduce-scatter.11.cloned.1.call-update) | async-done | bytes 1769488 | tf_op jit(solution)/shard_map/reduce_scatter | solution.py:281
  1616.8 91.4 %all-reduce.65.cloned.1.call-done = f32[3,128,128]{2,1,0:T(8,128)} async-done(((f32[3,128,128]{2,1,0:T(8,128)}), f32[3,128,128]{2,1,0:T(8,128)}) %all-reduce.65.cloned.1.call-update) | async-done | bytes 196624 | tf_op jit(solution)/shard_map/psum | solution.py:337
  1711.5 421.7 %all-reduce.67.cloned.1.call-done = (f32[2048,1536]{1,0:T(8,128)}, f32[2048,1536]{1,0:T(8,128)}) async-done(((f32[2048,1536]{1,0:T(8,128)}, f32[2048,1536]{1,0:T(8,128)}), (f32[2048,1536]{1,0:T(8,128)}, f32[2048,1536]{1,0:T(8,128)})) %all-reduce.67.cloned.1.call-update) | async-done | bytes 25165840 | tf_op jit(solution)/shard_map/psum | solution.py:240
  2141.9 37.5 %all-reduce.48 = (f32[1536]{0:T(1024)S(1)}, f32[6,768]{1,0:T(8,128)S(1)}, f32[5,64]{1,0:T(8,128)S(1)}, f32[3,12]{1,0:T(4,128)S(1)}) all-reduce(f32[1536]{0:T(1024)S(1)} %get-tuple-element.825, f32[6,768]{1,0:T(8,128)S(1)} %pad_maximum_fusion.5, f32[5,64]{1,0:T(8,128)S(1)} %pad_add_fusion, ...), channel_id=1, replica_groups=mesh['dp'=8,'mp'=4] {'dp'}, use_global_device_ids=true, to_apply=%region_41.42 | all-reduce | flops 6500 | bytes 52000 | tf_op jit(solution)/shard_map/psum | solution.py:290
  2216.4 14.9 reduce.108
  2244.7 20.8 fusion.146
  2265.4 15.5 all-to-all-done.1
  (1539 shorter events, 840.1 us)
Async XLA Ops:
  7.2 90.0 %all-gather.8.cloned.1.call-start = ((), (), s32[]{:S(2)}) async-start(), calls=%async_computation.7 | async-start | bytes 1310720 | tf_op jit(solution)/shard_map/all_gather | solution.py:233
  8.1 46.7 %copy-start.128 = (f32[64]{0:T(128)}, f32[64]{0:T(128)S(1)}, u32[]{:S(2)}) copy-start(f32[64]{0:T(128)S(1)} %get-tuple-element.965) | copy-start | bytes 772
  8.1 46.7 %copy-start.130 = (f32[64]{0:T(128)}, f32[64]{0:T(128)S(1)}, u32[]{:S(2)}) copy-start(f32[64]{0:T(128)S(1)} %get-tuple-element.966) | copy-start | bytes 772
  8.1 46.7 %copy-start.132 = (f32[64]{0:T(128)}, f32[64]{0:T(128)S(1)}, u32[]{:S(2)}) copy-start(f32[64]{0:T(128)S(1)} %get-tuple-element.963) | copy-start | bytes 772
  8.1 46.7 %copy-start.134 = (f32[64]{0:T(128)}, f32[64]{0:T(128)S(1)}, u32[]{:S(2)}) copy-start(f32[64]{0:T(128)S(1)} %get-tuple-element.964) | copy-start | bytes 772
  8.2 37.1 %copy-start.76 = (f32[1536]{0:T(1024)S(1)}, f32[1536]{0:T(1024)}, u32[]{:S(2)}) copy-start(f32[1536]{0:T(1024)} %param.30) | copy-start | bytes 18436
  12.3 37.3 %copy-start.78 = (f32[2048]{0:T(1024)}, f32[2048]{0:T(1024)S(1)}, u32[]{:S(2)}) copy-start(f32[2048]{0:T(1024)S(1)} %fusion.204) | copy-start | bytes 24580
  57.8 128.9 %all-gather.6.cloned.1.call-start = ((), (), s32[]{:S(2)}) async-start(), calls=%async_computation.6 | async-start | bytes 7962624 | tf_op jit(solution)/shard_map/all_gather | solution.py:213
  58.9 873.1 %reduce-scatter.13.cloned.1.call-start = ((), (), s32[]{:S(2)}) async-start(), calls=%async_computation.14 | async-start | bytes 2621440
  97.2 99.3 %slice-start = ((s8[6291456]{0:T(1024)(128)(4,1)}), s8[2097152]{0:T(1024)(128)(4,1)S(1)}, s32[]{:S(2)}) async-start(s8[6291456]{0:T(1024)(128)(4,1)} %bitcast.643), calls=%async_computation.18 | async-start | bytes 4194304
  902.9 96.2 %reduce-scatter.17.cloned.1.call-start = ((), (), s32[]{:S(2)}) async-start(), calls=%async_computation.16 | async-start | bytes 884736
  910.4 154.7 %reduce-scatter.15.cloned.1.call-start = ((), (), s32[]{:S(2)}) async-start(), calls=%async_computation.15 | async-start | bytes 884736
  942.3 57.7 %copy-start.113 = (f32[192,12]{0,1:T(8,128)S(1)}, f32[192,12]{0,1:T(8,128)}, u32[]{:S(2)}) copy-start(f32[192,12]{0,1:T(8,128)} %param.29) | copy-start | bytes 27652
  945.8 129.6 %copy-start.30 = (bf16[2048,768]{1,0:T(8,128)(2,1)S(1)}, bf16[2048,768]{1,0:T(8,128)(2,1)}, u32[]{:S(2)}) copy-start(bf16[2048,768]{1,0:T(8,128)(2,1)} %get-tuple-element.940) | copy-start | bytes 9437188
  945.8 199.3 %all-reduce.57.cloned.1.call-start = ((), (), s32[]{:S(2)}) async-start(), calls=%async_computation.9 | async-start | bytes 393216 | tf_op jit(solution)/shard_map/psum | solution.py:337
  1075.3 149.5 %all-reduce.59.cloned.1.call-start = ((), (), s32[]{:S(2)}) async-start(), calls=%async_computation.10 | async-start | bytes 393216 | tf_op jit(solution)/shard_map/psum | solution.py:337
  1084.5 68.6 %copy-start.36 = (f32[1,192,128]{1,2,0:T(8,128)S(1)}, f32[1,192,128]{1,2,0:T(8,128)}, u32[]{:S(2)}) copy-start(f32[1,192,128]{1,2,0:T(8,128)} %copy-done.35) | copy-start | bytes 294916
  1084.5 68.6 %copy-start.38 = (f32[1,192,128]{1,2,0:T(8,128)S(1)}, f32[1,192,128]{1,2,0:T(8,128)}, u32[]{:S(2)}) copy-start(f32[1,192,128]{1,2,0:T(8,128)} %copy-done.37) | copy-start | bytes 294916
  1155.0 143.4 %all-reduce.61.cloned.1.call-start = ((), (), s32[]{:S(2)}) async-start(), calls=%async_computation.11 | async-start | bytes 393216 | tf_op jit(solution)/shard_map/psum | solution.py:337
  1228.1 144.0 %all-reduce.63.cloned.1.call-start = ((), (), s32[]{:S(2)}) async-start(), calls=%async_computation.12 | async-start | bytes 393216 | tf_op jit(solution)/shard_map/psum | solution.py:337
  1301.6 303.3 %reduce-scatter.11.cloned.1.call-start = ((), (), s32[]{:S(2)}) async-start(), calls=%async_computation.8 | async-start | bytes 15925248 | tf_op jit(solution)/shard_map/reduce_scatter | solution.py:281
  1312.8 395.4 %all-reduce.65.cloned.1.call-start = ((), (), s32[]{:S(2)}) async-start(), calls=%async_computation.13 | async-start | bytes 393216 | tf_op jit(solution)/shard_map/psum | solution.py:337
  1375.2 758.0 %all-reduce.67.cloned.1.call-start = ((), (), s32[]{:S(2)}) async-start(), calls=%async_computation.17 | async-start | bytes 50331648 | tf_op jit(solution)/shard_map/psum | solution.py:240
  1612.5 570.0 %all-to-all-start = ((f32[5,8,192,64]{2,3,0,1:T(8,128)}), f32[5,8,192,64]{2,3,0,1:T(8,128)S(1)}, u32[]{:S(2)}, u32[]{:S(2)}) async-start(f32[5,8,192,64]{2,3,0,1:T(8,128)} %copy.677), calls=%async_computation.1 | async-start | bytes 5242880 | tf_op jit(solution)/shard_map/all_to_all | solution.py:318
  1616.7 93.5 %copy-start.98 = (f32[192,12]{0,1:T(8,128)S(1)}, f32[192,12]{0,1:T(8,128)}, u32[]{:S(2)}) copy-start(f32[192,12]{0,1:T(8,128)} %param.26) | copy-start | bytes 27652
  1616.7 94.2 %copy-start.69 = (f32[192,64]{0,1:T(8,128)S(1)}, f32[192,64]{0,1:T(8,128)}, u32[]{:S(2)}) copy-start(f32[192,64]{0,1:T(8,128)} %param.25) | copy-start | bytes 147460
  1616.7 516.5 %copy-start.77 = (f32[1536]{0:T(1024)S(1)}, f32[1536]{0:T(1024)}, u32[]{:S(2)}) copy-start(f32[1536]{0:T(1024)} %param.30) | copy-start | bytes 18436
  1616.7 516.5 %copy-start.79 = (f32[2048]{0:T(1024)S(1)}, f32[2048]{0:T(1024)}, u32[]{:S(2)}) copy-start(f32[2048]{0:T(1024)} %copy-done.78) | copy-start | bytes 24580
  2133.2 46.2 %copy-start.93 = (f32[3,12]{1,0:T(4,128)S(1)}, f32[3,12]{1,0:T(4,128)}, u32[]{:S(2)}) copy-start(f32[3,12]{1,0:T(4,128)} %get-tuple-element.1457) | copy-start | bytes 436
  2133.2 47.4 %copy-start.124 = (f32[5,64]{1,0:T(8,128)S(1)}, f32[5,64]{1,0:T(8,128)}, u32[]{:S(2)}) copy-start(f32[5,64]{1,0:T(8,128)} %param.32) | copy-start | bytes 3844
  2133.2 48.6 %copy-start.41 = (f32[5,768]{1,0:T(8,128)S(1)}, f32[5,768]{1,0:T(8,128)}, u32[]{:S(2)}) copy-start(f32[5,768]{1,0:T(8,128)} %get-tuple-element.1431) | copy-start | bytes 46084
  2239.0 41.9 %all-to-all-start.1 = ((f32[8,1,61440]{2,1,0:T(1,128)}), f32[8,1,61440]{2,1,0:T(1,128)S(1)}, u32[]{:S(2)}, u32[]{:S(2)}) async-start(f32[8,1,61440]{2,1,0:T(1,128)} %reshape.1293), calls=%async_computation.2 | async-start | bytes 3932160 | tf_op jit(solution)/shard_map/all_to_all | solution.py:320
  (351 other events, 1836.1 us)
Sparse Core Ops, SparseCore 0:
  57.9 17.6 all-gather.7
  78.4 108.2 all-gather.5
  903.0 28.9 reduce-scatter.12
  935.8 63.2 reduce-scatter.16
  1002.8 62.2 reduce-scatter.14
  1075.4 69.6 all-reduce.56
  1155.1 69.6 all-reduce.58
  1228.7 69.6 all-reduce.60
  1302.3 69.6 all-reduce.62
  1376.1 228.7 reduce-scatter.10
  1608.8 99.3 all-reduce.64
  1711.2 421.9 all-reduce.66
where the time goes:
time: 2330 us; the launch traced here: 2320 us
  waiting for transfers between devices  1160 us (50%)
  matrix products  400 us (17%)
  local copies, waits for them, and re-layouts  300 us (13%)
  other arithmetic  292 us (13%)
  blocking collectives  124 us (5%)
    psum x1, waiting for transfers between devices, body(): branch_sum = lax.psum(branch_part, 'mp')  422 us
    psum x5, waiting for transfers between devices, body(): lax.psum(jnp.einsum('kdp,kdq->kpq', current, current, precision=highest),...  295 us
    reduce_scatter x1, waiting for transfers between devices, body(): lax.psum_scatter(jnp.stack([grad_zed, grad_xin, grad_wout]), 'dp', scatte...  207 us
    dot_general x16, matrix products, mixer(): jnp.einsum('chts,cshp->cthp', weights, inputs, precision=highest)  136 us
    unnamed x15, waiting for transfers between devices  132 us
    all_gather x1, waiting for transfers between devices, body(): lax.all_gather(w_heads.astype(jnp.bfloat16), 'dp', axis=1, tiled=True)  86.8 us
  transfers between devices with their start and end apart: 14, of which 12 were waited for; matrix products, arithmetic and copies ran while one was open for 8% of the time, Pallas kernels for 0%

commit v1 on v0

v1 whole, which is shorter than its diff:
```python
import functools
import math

import jax
import jax.numpy as jnp
from jax import lax
from jax.experimental import pallas as pl
from jax.experimental.pallas import tpu as pltpu
from jax.sharding import PartitionSpec as P


D = 1536
CONV = 4
NS_STEPS = 5
INNER = 3072

eps_norm = 1e-05
ns_coeffs = (3.4445, -4.775, 2.0315)
momentum_beta = 0.95
muon_rate = 0.02
decay_rate = 0.1
adam_rate = 0.1
adam_first = 0.9
adam_second = 0.999
adam_steps = 2.0

f32 = jnp.float32
bf16 = jnp.bfloat16
HEADDIM = 64
STATE = 128
SPAN = 256
TILE = 128

NN = (((1,), (0,)), ((), ()))
NT = (((1,), (1,)), ((), ()))
TN = (((0,), (0,)), ((), ()))


def dot(lhs, rhs, dims=NN):
    return lax.dot_general(lhs, rhs, dims, preferred_element_type=f32)


def split(value):
    high = value.astype(bf16)
    return high, (value - high.astype(f32)).astype(bf16)


def sigmoid(value):
    return 0.5 + 0.5 * jnp.tanh(0.5 * value)


def shift_right(value, amount):
    return pltpu.roll(value, amount, axis=1)


def shift_left(value, amount):
    return pltpu.roll(value, value.shape[1] - amount, axis=1)


def lane_iota(shape):
    return lax.broadcasted_iota(jnp.int32, shape, len(shape) - 1)


def conv_masks(seg):
    at = lane_iota(seg.shape)
    return [
        jnp.where((shift_right(seg, k) == seg) & (at >= k), 1.0, 0.0).astype(f32)[:1]
        for k in (1, 2, 3)
    ]


def segment_scan(value, seg, reach):
    at = lane_iota(value.shape)
    step = 1
    while step < reach:
        linked = (shift_right(seg, step) == seg) & (at >= step)
        value = value + jnp.where(linked, shift_right(value, step), 0.0)
        step *= 2
    return value


def segment_scan_back(value, seg, reach):
    length = value.shape[1]
    at = lane_iota(value.shape)
    step = 1
    while step < reach:
        linked = (shift_left(seg, step) == seg) & (at < length - step)
        value = value + jnp.where(linked, shift_left(value, step), 0.0)
        step *= 2
    return value


def head_rows(step_raw, seg, headcol):
    biased = step_raw + headcol[:, 1:2]
    dt = jnp.maximum(biased, 0.0) + jnp.log1p(jnp.exp(-jnp.abs(biased)))
    rate = -jnp.exp(headcol[:, 0:1])
    cum = segment_scan(rate * dt, seg, SPAN)
    last_cum = cum[:, SPAN - 1 : SPAN]
    last_seg = seg[:, SPAN - 1 : SPAN]
    same = seg == last_seg
    at = lane_iota(cum.shape)
    tail = jnp.exp(jnp.where(same & (at < SPAN), last_cum - cum, -1e30))
    head = jnp.exp(jnp.where(same & (at >= SPAN), cum - last_cum, -1e30))
    return biased, dt, rate, cum, tail, head


def decay_tile(cum_row, cum_col, s0, t0):
    gap = cum_row[:, t0 : t0 + TILE] - cum_col[s0 // TILE]
    return jnp.exp(jnp.minimum(gap, 0.0))


def tiles_of(block):
    base = block * SPAN
    return ((base, base), (base, base + TILE), (base + TILE, base + TILE))


def score_tiles(bc, seg, seg_col, score_ref):
    row = lax.broadcasted_iota(jnp.int32, (TILE, TILE), 0)
    col = lax.broadcasted_iota(jnp.int32, (TILE, TILE), 1)
    for block in range(2):
        base = block * SPAN
        full = dot(bc[:STATE, base : base + SPAN], bc[STATE:, base : base + SPAN], TN)
        for index, (s0, t0) in enumerate(tiles_of(block)):
            part = full[s0 - base : s0 - base + TILE, t0 - base : t0 - base + TILE]
            ok = seg_col[s0 // TILE] == seg[:1, t0 : t0 + TILE]
            if s0 == t0:
                ok = ok & (row <= col)
            score_ref[block * 3 + index] = jnp.where(ok, part, 0.0)


def column_of(row8):
    return [
        jnp.broadcast_to(row8[:1, s0 : s0 + TILE], (TILE, TILE)).T
        for s0 in range(0, row8.shape[1], TILE)
    ]


def conv_of(raw, taps, masks):
    shifted = [shift_right(raw, k + 1) * masks[k] for k in range(3)]
    pre = taps[4] + taps[3] * raw + taps[2] * shifted[0] + taps[1] * shifted[1] + taps[0] * shifted[2]
    return pre, shifted


def square_of(tiles):
    zero = jnp.zeros_like(tiles[0])
    return jnp.concatenate(
        [jnp.concatenate([tiles[0], tiles[1]], axis=1), jnp.concatenate([zero, tiles[2]], axis=1)],
        axis=0,
    )


def forward_kernel(heads, raw_ref, step_ref, bc_ref, seg_ref, taps_ref, headcol_ref, skip_ref,
                   y_ref, state_ref, score_ref, rows_ref):
    length = raw_ref.shape[1]
    seg = jnp.broadcast_to(seg_ref[0], (8, length))
    bc = bc_ref[...]
    seg_col = column_of(seg.astype(f32))
    score_tiles(bc, seg.astype(f32), seg_col, score_ref)
    masks = conv_masks(seg)
    seg16 = jnp.broadcast_to(seg_ref[0], (step_ref.shape[0], length))
    _, dt, _, cum, tail, head = head_rows(step_ref[...], seg16, headcol_ref[...])
    rows_ref[0] = dt
    rows_ref[1] = cum
    rows_ref[2] = tail
    rows_ref[3] = head

    def per_head(h, carry):
        rows = pl.ds(pl.multiple_of(h * HEADDIM, HEADDIM), HEADDIM)
        raw = raw_ref[rows, :]
        taps_all = taps_ref[rows, :]
        taps = [taps_all[:, k : k + 1] for k in range(5)]
        pre, _ = conv_of(raw, taps, masks)
        xc = pre * sigmoid(pre)
        dt_row = rows_ref[0, pl.ds(h, 1), :]
        cum_row = rows_ref[1, pl.ds(h, 1), :]
        xbar = xc * dt_row
        xh, xl = split(xbar)
        cum_col = column_of(jnp.broadcast_to(cum_row, (8, length)))
        parts = []
        for block in range(2):
            base = block * SPAN
            tiles = [
                decay_tile(cum_row, cum_col, s0, t0) * score_ref[block * 3 + i]
                for i, (s0, t0) in enumerate(tiles_of(block))
            ]
            halves = [split(tile) for tile in tiles]
            wh = square_of([p[0] for p in halves])
            wl = square_of([p[1] for p in halves])
            bxh, bxl = xh[:, base : base + SPAN], xl[:, base : base + SPAN]
            both = dot(jnp.concatenate([bxh, bxl], axis=0), wh)
            parts.append(both[:HEADDIM] + both[HEADDIM:] + dot(bxh, wl))
        tail_row = rows_ref[2, pl.ds(h, 1), :]
        head_row = rows_ref[3, pl.ds(h, 1), :]
        th, tl = split(xbar[:, :SPAN] * tail_row[:, :SPAN])
        both = dot(jnp.concatenate([th, tl], axis=0), bc[:STATE, :SPAN], NT)
        state = both[:HEADDIM] + both[HEADDIM:]
        state_ref[0, rows, :] = state
        sh, sl = split(state)
        both = dot(jnp.concatenate([sh, sl], axis=0), bc[STATE:, SPAN:])
        cross = (both[:HEADDIM] + both[HEADDIM:]) * head_row[:, SPAN:]
        skip = skip_ref[2, h]
        y_ref[rows, :SPAN] = parts[0] + skip * xc[:, :SPAN]
        y_ref[rows, SPAN:] = parts[1] + cross + skip * xc[:, SPAN:]
        return carry

    lax.fori_loop(0, heads, per_head, 0, unroll=4)


def backward_kernel(first_head, heads, raw_ref, z_ref, y_ref, do_ref, step_ref, bc_ref, seg_ref, norm_ref,
                    state_ref, taps_ref, headcol_ref, skip_ref,
                    dzx_ref, dstep_ref, dbc_ref, gsum_ref, ghead_ref,
                    score_ref, rows_ref, dscore_ref, sums_ref, dcross_ref, gconv_ref):
    item = pl.program_id(0)
    length = raw_ref.shape[1]
    seg = jnp.broadcast_to(seg_ref[0], (8, length))
    bc = bc_ref[...]
    seg_col = column_of(seg.astype(f32))
    score_tiles(bc, seg.astype(f32), seg_col, score_ref)
    masks = conv_masks(seg)
    seg16 = jnp.broadcast_to(seg_ref[0], (step_ref.shape[0], length))
    headcol = headcol_ref[...]
    biased, dt, rate, cum, tail, head = head_rows(step_ref[...], seg16, headcol)
    rows_ref[0] = dt
    rows_ref[1] = cum
    rows_ref[2] = tail
    rows_ref[3] = head
    dscore_ref[...] = jnp.zeros_like(dscore_ref)
    dcross_ref[...] = jnp.zeros_like(dcross_ref)
    sums_ref[...] = jnp.zeros_like(sums_ref)

    @pl.when(item == 0)
    def _():
        gconv_ref[...] = jnp.zeros_like(gconv_ref)
        ghead_ref[...] = jnp.zeros_like(ghead_ref)

    inv_row = norm_ref[0, 0:1, :]
    pull_row = norm_ref[0, 1:2, :]

    def fold(value):
        total = value[:, :TILE]
        for start in range(TILE, length, TILE):
            total = total + value[:, start : start + TILE]
        return total

    def per_head(h, carry):
        rows = pl.ds(pl.multiple_of(h * HEADDIM, HEADDIM), HEADDIM)
        one = pl.ds(first_head + h, 1)
        x_rows = pl.ds(pl.multiple_of((heads + h) * HEADDIM, HEADDIM), HEADDIM)
        taps_all = taps_ref[rows, :]
        taps = [taps_all[:, k : k + 1] for k in range(5)]
        gain = taps_all[:, 5:6]
        skip = skip_ref[2, first_head + h]
        z = z_ref[rows, :]
        y = y_ref[rows, :]
        d_o = do_ref[rows, :]
        sig_z = sigmoid(z)
        silu_z = z * sig_z
        v = y * silu_z
        dor = d_o * inv_row
        gconv_ref[5, rows, :] += fold(dor * v)
        d_v = dor * gain - v * pull_row
        dzx_ref[rows, :] = (d_v * y * (sig_z * (1.0 + z * (1.0 - sig_z)))).astype(bf16)
        dy = d_v * silu_z
        raw = raw_ref[rows, :]
        pre, shifted = conv_of(raw, taps, masks)
        sig_p = sigmoid(pre)
        xc = pre * sig_p
        dt_row = rows_ref[0, one, :]
        cum_row = rows_ref[1, one, :]
        xbar = xc * dt_row
        sums_ref[0, one, :] = jnp.sum(dy * y, axis=0, keepdims=True)
        sums_ref[1, one, :] = jnp.sum(dy * xc, axis=0, keepdims=True)
        xh, xl = split(xbar)
        yh, yl = split(dy)
        cum_col = column_of(jnp.broadcast_to(cum_row, (8, length)))
        x3 = jnp.concatenate([xh, xl, xh], axis=0)
        y3 = jnp.concatenate([yh, yh, yl], axis=0)
        parts = []
        for block in range(2):
            base = block * SPAN
            decays = [decay_tile(cum_row, cum_col, s0, t0) for s0, t0 in tiles_of(block)]
            halves = [split(decays[i] * score_ref[block * 3 + i]) for i in range(3)]
            wh = square_of([p[0] for p in halves])
            wl = square_of([p[1] for p in halves])
            byh, byl = yh[:, base : base + SPAN], yl[:, base : base + SPAN]
            both = dot(jnp.concatenate([byh, byl], axis=0), wh, NT)
            parts.append(both[:HEADDIM] + both[HEADDIM:] + dot(byh, wl, NT))
            top = dot(x3[:, base : base + TILE], y3[:, base : base + SPAN], TN)
            low = dot(x3[:, base + TILE : base + SPAN], y3[:, base + TILE : base + SPAN], TN)
            dscore_ref[block * 3] += decays[0] * top[:, :TILE]
            dscore_ref[block * 3 + 1] += decays[1] * top[:, TILE:]
            dscore_ref[block * 3 + 2] += decays[2] * low
        tail_row = rows_ref[2, one, :SPAN]
        head_row = rows_ref[3, one, :][:, SPAN:]
        dyu = dy[:, SPAN:] * head_row
        uh, ul = split(dyu)
        both = dot(jnp.concatenate([uh, ul], axis=0), bc[STATE:, SPAN:], NT)
        dstate = both[:HEADDIM] + both[HEADDIM:]
        dsh, dsl = split(dstate)
        both = dot(jnp.concatenate([dsh, dsl], axis=0), bc[:STATE, :SPAN])
        first = parts[0] + (both[:HEADDIM] + both[HEADDIM:]) * tail_row
        sh, sl = split(state_ref[0, rows, :])
        dcross_ref[1] += dot(jnp.concatenate([sh, sh, sl], axis=0), jnp.concatenate([uh, ul, uh], axis=0), TN)
        wxh, wxl = split(xbar[:, :SPAN] * tail_row)
        dcross_ref[0] += dot(jnp.concatenate([dsh, dsh, dsl], axis=0), jnp.concatenate([wxh, wxl, wxh], axis=0), TN)
        dxbar = jnp.concatenate([first, parts[1]], axis=1)
        sums_ref[2, one, :] = jnp.sum(dxbar * xc, axis=0, keepdims=True)
        dpre = (dxbar * dt_row + skip * dy) * (sig_p * (1.0 + pre * (1.0 - sig_p)))
        gconv_ref[4, rows, :] += fold(dpre)
        gconv_ref[3, rows, :] += fold(dpre * raw)
        dx = taps[3] * dpre
        for k in range(3):
            gconv_ref[2 - k, rows, :] += fold(dpre * shifted[k])
            dx = dx + taps[2 - k] * shift_left(dpre * masks[k], k + 1)
        dzx_ref[x_rows, :] = dx.astype(bf16)
        return carry

    lax.fori_loop(0, heads, per_head, 0, unroll=2)

    row = lax.broadcasted_iota(jnp.int32, (TILE, TILE), 0)
    col = lax.broadcasted_iota(jnp.int32, (TILE, TILE), 1)
    segf = seg.astype(f32)
    for block in range(2):
        base = block * SPAN
        halves = []
        for i, (s0, t0) in enumerate(tiles_of(block)):
            ok = seg_col[s0 // TILE] == segf[:1, t0 : t0 + TILE]
            if s0 == t0:
                ok = ok & (row <= col)
            halves.append(split(jnp.where(ok, dscore_ref[block * 3 + i], 0.0)))
        dh = square_of([p[0] for p in halves])
        dl = square_of([p[1] for p in halves])
        b_part = bc[:STATE, base : base + SPAN]
        c_part = bc[STATE:, base : base + SPAN]
        d_c = dot(b_part, dh) + dot(b_part, dl)
        d_b = dot(c_part, dh, NT) + dot(c_part, dl, NT)
        if block == 0:
            d_b = d_b + dcross_ref[0]
        else:
            d_c = d_c + dcross_ref[1]
        dbc_ref[:STATE, base : base + SPAN] = d_b
        dbc_ref[STATE:, base : base + SPAN] = d_c
    skipcol = headcol[:, 2:3]
    p_y, p_x, p_b = sums_ref[0], sums_ref[1], sums_ref[2]
    d_cum = p_y - skipcol * p_x - rows_ref[0] * p_b
    d_a = segment_scan_back(d_cum, seg16, SPAN)
    d_step = (p_b + d_a * rate) * sigmoid(biased)
    dstep_ref[...] = d_step.astype(bf16)
    ghead_ref[0] += fold(d_a * rate * rows_ref[0])
    ghead_ref[1] += fold(d_step)
    ghead_ref[2] += fold(p_x)

    @pl.when(item == pl.num_programs(0) - 1)
    def _():
        for index in range(6):
            gsum_ref[:, index : index + 1] = jnp.sum(gconv_ref[index], axis=1, keepdims=True)


def run_forward(first, count, before, raw, small, step_row, bc, seg, taps, headcol, head_par):
    seqs, _, length = seg.shape
    heads = head_par.shape[1]
    inner = heads * HEADDIM
    before = [] if before is None else list(before)

    def kernel(*refs):
        forward_kernel(heads, *refs[: 7], *refs[7 + len(before) :])

    grid_spec = pl.GridSpec(
        grid=(count,),
        in_specs=[
            pl.BlockSpec((inner, length), lambda i: (0, first + i)),
            pl.BlockSpec((16, length), lambda i: (step_row // 16, first + i)),
            pl.BlockSpec((2 * STATE, length), lambda i: (0, first + i)),
            pl.BlockSpec((1, 1, length), lambda i: (first + i, 0, 0)),
            pl.BlockSpec(taps.shape, lambda i: (0, 0)),
            pl.BlockSpec(headcol.shape, lambda i: (0, 0)),
            pl.BlockSpec(memory_space=pltpu.SMEM),
        ]
        + [pl.BlockSpec(memory_space=pl.ANY)] * len(before),
        out_specs=[
            pl.BlockSpec((inner, length), lambda i: (0, first + i)),
            pl.BlockSpec((1, inner, STATE), lambda i: (first + i, 0, 0)),
        ],
        scratch_shapes=[pltpu.VMEM((6, TILE, TILE), f32), pltpu.VMEM((4, 16, length), f32)],
    )
    return pl.pallas_call(
        kernel,
        grid_spec=grid_spec,
        out_shape=[
            jax.ShapeDtypeStruct((inner, seqs * length), f32),
            jax.ShapeDtypeStruct((seqs, inner, STATE), f32),
        ],
        input_output_aliases={7 + index: index for index in range(len(before))},
        compiler_params=pltpu.CompilerParams(vmem_limit_bytes=24 * 2**20),
    )(raw, small, bc, seg, taps, headcol, head_par, *before)


def run_backward(part, parts, raw, z, y, d_o, small, step_row, bc, seg, norm_rows, state, taps, headcol, head_par):
    seqs, _, length = seg.shape
    heads = head_par.shape[1] // parts
    inner = heads * HEADDIM
    big = pl.BlockSpec((inner, length), lambda i: (part, i))
    grid_spec = pl.GridSpec(
        grid=(seqs,),
        in_specs=[
            big, big, big, big,
            pl.BlockSpec((16, length), lambda i: (step_row // 16, i)),
            pl.BlockSpec((2 * STATE, length), lambda i: (0, i)),
            pl.BlockSpec((1, 1, length), lambda i: (i, 0, 0)),
            pl.BlockSpec((1, 2, length), lambda i: (i, 0, 0)),
            pl.BlockSpec((1, inner, STATE), lambda i: (i, part, 0)),
            pl.BlockSpec((inner, taps.shape[1]), lambda i: (part, 0)),
            pl.BlockSpec(headcol.shape, lambda i: (0, 0)),
            pl.BlockSpec(memory_space=pltpu.SMEM),
        ],
        out_specs=[
            pl.BlockSpec((2 * inner, length), lambda i: (0, i)),
            pl.BlockSpec((16, length), lambda i: (0, i)),
            pl.BlockSpec((2 * STATE, length), lambda i: (0, i)),
            pl.BlockSpec((inner, 8), lambda i: (0, 0)),
            pl.BlockSpec((3, 16, TILE), lambda i: (0, 0, 0)),
        ],
        scratch_shapes=[
            pltpu.VMEM((6, TILE, TILE), f32),
            pltpu.VMEM((4, 16, length), f32),
            pltpu.VMEM((6, TILE, TILE), f32),
            pltpu.VMEM((3, 16, length), f32),
            pltpu.VMEM((2, STATE, SPAN), f32),
            pltpu.VMEM((6, inner, TILE), f32),
        ],
    )
    tok = seqs * length
    return pl.pallas_call(
        functools.partial(backward_kernel, part * heads, heads),
        grid_spec=grid_spec,
        out_shape=[
            jax.ShapeDtypeStruct((2 * inner, tok), bf16),
            jax.ShapeDtypeStruct((16, tok), bf16),
            jax.ShapeDtypeStruct((2 * STATE, tok), f32),
            jax.ShapeDtypeStruct((inner, 8), f32),
            jax.ShapeDtypeStruct((3, 16, TILE), f32),
        ],
        compiler_params=pltpu.CompilerParams(vmem_limit_bytes=32 * 2**20),
    )(raw, z, y, d_o, small, bc, seg, norm_rows, state, taps, headcol, head_par)


def gate_sums_kernel(y_ref, z_ref, do_ref, taps_ref, sums_ref):
    z = z_ref[...]
    v = y_ref[...] * (z * sigmoid(z))
    gain = taps_ref[:, 5:6]
    sums_ref[0:1, :] = jnp.sum(v * v, axis=0, keepdims=True)
    sums_ref[1:2, :] = jnp.sum(do_ref[...] * gain * v, axis=0, keepdims=True)


def run_gate_sums(y, z, d_o, taps):
    inner, tok = y.shape
    block = 2 * SPAN
    big = pl.BlockSpec((inner, block), lambda i: (0, i))
    return pl.pallas_call(
        gate_sums_kernel,
        grid=(tok // block,),
        in_specs=[big, big, big, pl.BlockSpec(taps.shape, lambda i: (0, 0))],
        out_specs=pl.BlockSpec((2, block), lambda i: (0, i)),
        out_shape=jax.ShapeDtypeStruct((2, tok), f32),
    )(y, z, d_o, taps)


def gate_out_kernel(chip_ref, y_ref, z_ref, inv_ref, taps_ref, out_ref, send_ref):
    z = z_ref[...]
    v = y_ref[...] * (z * sigmoid(z))
    out = (v * inv_ref[0:1, :] * taps_ref[:, 5:6]).astype(bf16)
    out_ref[...] = out

    @pl.when(pl.program_id(0) < pl.num_programs(0) // 2)
    def _():
        send_ref[...] = out


def run_gate_out(y, z, inv, taps, chip):
    inner, tok = y.shape
    block = 2 * SPAN
    steps = tok // block
    half = steps // 2

    def at(i, chip_ref):
        return 0, lax.rem(i + (1 - chip_ref[0]) * half, steps)

    big = pl.BlockSpec((inner, block), at)
    return pl.pallas_call(
        gate_out_kernel,
        grid_spec=pltpu.PrefetchScalarGridSpec(
            num_scalar_prefetch=1,
            grid=(steps,),
            in_specs=[
                big,
                big,
                pl.BlockSpec((1, block), at),
                pl.BlockSpec(taps.shape, lambda i, chip_ref: (0, 0)),
            ],
            out_specs=[
                big,
                pl.BlockSpec((inner, block), lambda i, chip_ref: (0, jnp.minimum(i, half - 1))),
            ],
        ),
        out_shape=[
            jax.ShapeDtypeStruct((inner, tok), bf16),
            jax.ShapeDtypeStruct((inner, tok // 2), bf16),
        ],
    )(chip.reshape(1), y, z, inv, taps)


def state_forward_kernel(raw_ref, seg_ref, taps_ref, out_ref):
    seg = jnp.broadcast_to(seg_ref[0], (8, raw_ref.shape[1]))
    taps_all = taps_ref[...]
    pre, _ = conv_of(raw_ref[...], [taps_all[:, k : k + 1] for k in range(5)], conv_masks(seg))
    out_ref[...] = (pre * sigmoid(pre)).astype(bf16)


def state_backward_kernel(raw_ref, grad_ref, seg_ref, taps_ref, out_ref, gpar_ref):
    length = raw_ref.shape[1]
    seg = jnp.broadcast_to(seg_ref[0], (8, length))
    masks = conv_masks(seg)
    taps_all = taps_ref[...]
    taps = [taps_all[:, k : k + 1] for k in range(5)]
    raw = raw_ref[...]
    pre, shifted = conv_of(raw, taps, masks)
    sig = sigmoid(pre)
    dpre = grad_ref[...] * (sig * (1.0 + pre * (1.0 - sig)))

    @pl.when(pl.program_id(0) == 0)
    def _():
        gpar_ref[...] = jnp.zeros_like(gpar_ref)

    def fold(value):
        total = value[:, :TILE]
        for start in range(TILE, length, TILE):
            total = total + value[:, start : start + TILE]
        return total

    gpar_ref[4] += fold(dpre)
    gpar_ref[3] += fold(dpre * raw)
    dx = taps[3] * dpre
    for k in range(3):
        gpar_ref[2 - k] += fold(dpre * shifted[k])
        dx = dx + taps[2 - k] * shift_left(dpre * masks[k], k + 1)
    out_ref[...] = dx.astype(bf16)


def run_state_forward(proj, row, seg, taps):
    seqs, _, length = seg.shape
    width = taps.shape[0]
    return pl.pallas_call(
        state_forward_kernel,
        grid=(seqs,),
        in_specs=[
            pl.BlockSpec((width, length), lambda i: (row // width, i)),
            pl.BlockSpec((1, 1, length), lambda i: (i, 0, 0)),
            pl.BlockSpec(taps.shape, lambda i: (0, 0)),
        ],
        out_specs=pl.BlockSpec((width, length), lambda i: (0, i)),
        out_shape=jax.ShapeDtypeStruct((width, seqs * length), bf16),
    )(proj, seg, taps)


def run_state_backward(proj, row, grad, seg, taps):
    seqs, _, length = seg.shape
    width = taps.shape[0]
    return pl.pallas_call(
        state_backward_kernel,
        grid=(seqs,),
        in_specs=[
            pl.BlockSpec((width, length), lambda i: (row // width, i)),
            pl.BlockSpec((width, length), lambda i: (0, i)),
            pl.BlockSpec((1, 1, length), lambda i: (i, 0, 0)),
            pl.BlockSpec(taps.shape, lambda i: (0, 0)),
        ],
        out_specs=[
            pl.BlockSpec((width, length), lambda i: (0, i)),
            pl.BlockSpec((5, width, TILE), lambda i: (0, 0, 0)),
        ],
        out_shape=[
            jax.ShapeDtypeStruct((width, seqs * length), bf16),
            jax.ShapeDtypeStruct((5, width, TILE), f32),
        ],
    )(proj, grad, seg, taps)


def product3(left, right):
    lh, ll = split(left)
    rh, rl = split(right)
    return dot(
        jnp.concatenate([lh, lh, ll], axis=1), jnp.concatenate([rh, rl, rh], axis=0)
    )


def gram3(value):
    high, low = split(value)
    cross = dot(high, low, TN)
    return dot(high, high, TN) + cross + cross.T


def grad_kernel(place_ref, left_ref, *refs):
    right_refs, keep_ref, send_ref, both_ref = refs[:-3], refs[-3], refs[-2], refs[-1]
    groups, rows = keep_ref.shape[:2]
    left = left_ref[...]
    at = 0
    for right_ref in right_refs:
        width = right_ref.shape[0]
        part = dot(right_ref[...], left).T
        for group in range(groups):
            for side in range(2):
                start = (2 * group + side) * rows
                both_ref[side, group, :, at : at + width] = part[start : start + rows]
        at += width
    mine = place_ref[0]
    keep_ref[...] = both_ref[mine]
    send_ref[...] = both_ref[1 - mine].astype(send_ref.dtype)


def run_grad(left, rights, narrow):
    count = lax.axis_size("dp")
    tok, features = left.shape
    rows = features // count
    lanes = 3 * TILE
    groups = lanes // (2 * rows)
    cols = sum(height for _, height, _ in rights)

    def right_spec(height, index):
        return pl.BlockSpec((height, tok), lambda i, place_ref: (index, 0))

    piece = pl.BlockSpec((groups, rows, cols), lambda i, place_ref: (i, 0, 0))
    return pl.pallas_call(
        grad_kernel,
        grid_spec=pltpu.PrefetchScalarGridSpec(
            num_scalar_prefetch=1,
            grid=(features // lanes,),
            in_specs=[pl.BlockSpec((tok, lanes), lambda i, place_ref: (0, i))]
            + [right_spec(height, index) for _, height, index in rights],
            out_specs=[piece, piece],
            scratch_shapes=[pltpu.VMEM((2, groups, rows, cols), f32)],
        ),
        out_shape=[
            jax.ShapeDtypeStruct((count // 2, rows, cols), f32),
            jax.ShapeDtypeStruct((count // 2, rows, cols), bf16 if narrow else f32),
        ],
        compiler_params=pltpu.CompilerParams(vmem_limit_bytes=24 * 2**20),
    )(lax.rem(lax.axis_index("dp"), 2).reshape(1), left, *[array for array, _, _ in rights])


def pair_kernel(place_ref, keep_ref, got_ref, *outs):
    total = keep_ref[0] + got_ref[0].astype(f32)
    for index, out_ref in enumerate(outs):

        @pl.when(pl.program_id(0) == index)
        def _(out_ref=out_ref):
            out_ref[...] = total.astype(out_ref.dtype)


def run_pair(keep, got, narrow):
    groups, rows, cols = keep.shape
    kinds = [bf16 if narrow and distance > 1 else f32 for distance in range(groups)]

    def at(i, place_ref):
        return place_ref[0] ^ i, 0, 0

    block = pl.BlockSpec((1, rows, cols), at)
    return pl.pallas_call(
        pair_kernel,
        grid_spec=pltpu.PrefetchScalarGridSpec(
            num_scalar_prefetch=1,
            grid=(groups,),
            in_specs=[block, block],
            out_specs=[pl.BlockSpec((rows, cols), lambda i, place_ref: (0, 0))] * groups,
        ),
        out_shape=[jax.ShapeDtypeStruct((rows, cols), kind) for kind in kinds],
    )((lax.axis_index("dp") // 2).reshape(1), keep, got)


def summed(part_refs, cols):
    total = part_refs[0][:, cols]
    for part_ref in part_refs[1:]:
        total = total + part_ref[:, cols].astype(f32)
    return total


def momentum_kernel(count, first, extra, *refs):
    groups = (refs[:count], refs[count : 2 * count])
    refs = refs[2 * count :]
    mom_ref = refs[0]
    outs = refs[-5:] if extra else refs[-3:]
    grad_ref, new_ref, gram_ref = outs[:3]
    left = lane_iota((HEADDIM, TILE)) < HEADDIM
    for group, part_refs in enumerate(groups):

        @pl.when((pl.program_id(0) >= first) == bool(group))
        def _(part_refs=part_refs):
            for pair in range(mom_ref.shape[2] // TILE):
                cols = slice(pair * TILE, (pair + 1) * TILE)
                grad = summed(part_refs, cols)
                new = momentum_beta * mom_ref[0, :, cols] + grad
                grad_ref[0, :, cols] = grad
                new_ref[0, :, cols] = new
                gram = gram3(new)
                gram_ref[pair] = jnp.where(left, gram[:HEADDIM], gram[HEADDIM:])

    if extra:
        grad = summed([ref for ref in refs[1 : 1 + count]], slice(0, TILE))
        outs[3][...] = grad
        outs[4][...] = momentum_beta * refs[1 + count][...] + grad


def run_momentum(groups, mom, where, before, small_mom):
    _, rows, cols = mom.shape
    width = cols // 2
    pairs = width // TILE
    steps, place = where
    first = groups[0][0].shape[1] // width
    count = len(groups[0])
    extra = small_mom is not None
    before = [] if before is None else list(before)
    at = pl.BlockSpec((1, rows, width), place)
    small = pl.BlockSpec((rows, TILE), lambda i: (0, 0))

    def part_spec(lowest, highest):
        return pl.BlockSpec((rows, width), lambda i: (0, jnp.clip(i - lowest, 0, highest)))

    in_specs = [part_spec(0, first - 1)] * count + [part_spec(first, steps - first - 1)] * count + [at]
    arrays = [*groups[0], *groups[1], mom]
    if extra:
        behind = (steps - first) * pairs
        in_specs += [pl.BlockSpec((rows, TILE), lambda i: (0, behind))] * count + [small]
        arrays += [*groups[1], small_mom]
    aliases = {len(arrays) + index: index for index in range(len(before))}
    return pl.pallas_call(
        functools.partial(momentum_kernel, count, first, extra),
        grid=(steps,),
        in_specs=in_specs + [pl.BlockSpec(memory_space=pl.ANY)] * len(before),
        out_specs=[at, at, pl.BlockSpec((pairs, HEADDIM, TILE), lambda i: (i, 0, 0))] + [small] * (2 * extra),
        out_shape=[
            jax.ShapeDtypeStruct(mom.shape, f32),
            jax.ShapeDtypeStruct(mom.shape, f32),
            jax.ShapeDtypeStruct((steps * pairs, HEADDIM, TILE), f32),
        ]
        + [jax.ShapeDtypeStruct((rows, TILE), f32)] * (2 * extra),
        input_output_aliases=aliases,
    )(*arrays, *before)


def sweep(grams, norms):
    row = lax.broadcasted_iota(jnp.int32, (TILE, TILE), 0)
    col = lax.broadcasted_iota(jnp.int32, (TILE, TILE), 1)
    eye = jnp.where(row == col, 1.0, 0.0).astype(f32)
    scales = [1.0 / (norm + 1e-07) for norm in norms]
    currents = [gram * scale * scale for gram, scale in zip(grams, scales)]
    factors = None
    for step in range(NS_STEPS):
        squares = [product3(current, current) for current in currents]
        polys = [
            ns_coeffs[0] * eye + ns_coeffs[1] * current + ns_coeffs[2] * square
            for current, square in zip(currents, squares)
        ]
        if factors is None:
            factors = polys
        else:
            factors = [product3(factor, poly) for factor, poly in zip(factors, polys)]
        if step < NS_STEPS - 1:
            halves = [product3(current, poly) for current, poly in zip(currents, polys)]
            currents = [product3(poly, half) for poly, half in zip(polys, halves)]
    return [factor * scale for factor, scale in zip(factors, scales)]


def head_factor_kernel(gram_ref, got_ref, out_ref):
    left = lane_iota((HEADDIM, TILE)) < HEADDIM
    first = lane_iota((1, TILE)) < HEADDIM
    row = lax.broadcasted_iota(jnp.int32, (TILE, TILE), 0)
    col = lax.broadcasted_iota(jnp.int32, (TILE, TILE), 1)
    grams, norms = [], []
    for pair in range(gram_ref.shape[0]):
        packed = gram_ref[pair] + got_ref[pair]
        gram = jnp.concatenate(
            [jnp.where(left, packed, 0.0), jnp.where(left, 0.0, packed)], axis=0
        )
        diag = jnp.sum(jnp.where(row == col, gram, 0.0), axis=0, keepdims=True)
        low = jnp.sum(jnp.where(first, diag, 0.0), axis=1, keepdims=True)
        high = jnp.sum(jnp.where(first, 0.0, diag), axis=1, keepdims=True)
        grams.append(gram)
        norms.append(jnp.sqrt(jnp.where(first, low, high)))
    for pair, factor in enumerate(sweep(grams, norms)):
        out_ref[pair] = factor


def full_factor_kernel(gram_ref, got_ref, out_ref):
    row = lax.broadcasted_iota(jnp.int32, (TILE, TILE), 0)
    col = lax.broadcasted_iota(jnp.int32, (TILE, TILE), 1)
    grams, norms = [], []
    for block in range(gram_ref.shape[0]):
        gram = gram_ref[block] + got_ref[block]
        diag = jnp.sum(jnp.where(row == col, gram, 0.0), axis=0, keepdims=True)
        grams.append(gram)
        norms.append(jnp.broadcast_to(jnp.sqrt(jnp.sum(diag, axis=1, keepdims=True)), (1, TILE)))
    for block, factor in enumerate(sweep(grams, norms)):
        out_ref[block] = factor


def run_factor(gram, got, kernel):
    count = gram.shape[0]
    return pl.pallas_call(kernel, out_shape=jax.ShapeDtypeStruct((count, TILE, TILE), f32))(gram, got)


def apply_kernel(weight_ref, mom_ref, factor_ref, *refs):
    out_ref = refs[-1]
    for block in range(factor_ref.shape[0]):
        cols = slice(block * TILE, (block + 1) * TILE)
        ortho = product3(mom_ref[0, :, cols], factor_ref[block])
        weight = weight_ref[0, :, cols]
        out_ref[0, :, cols] = weight - muon_rate * (
            0.2 * math.sqrt(D) * ortho + decay_rate * weight
        )


def run_apply(weight, mom, factor, where, before):
    _, rows, cols = mom.shape
    width = cols // 2
    before = [] if before is None else [before]
    at = pl.BlockSpec((1, rows, width), where[1])
    return pl.pallas_call(
        apply_kernel,
        grid=(where[0],),
        in_specs=[at, at, pl.BlockSpec((width // TILE, TILE, TILE), lambda i: (i, 0, 0))]
        + [pl.BlockSpec(memory_space=pl.ANY)] * len(before),
        out_specs=at,
        out_shape=jax.ShapeDtypeStruct(weight.shape, f32),
        input_output_aliases={3: 0} if before else {},
    )(weight, mom, factor, *before)


def small_blocks(own, near, far, across, heads):
    lanes = lane_iota(own.shape)
    both = jnp.where(lanes < HEADDIM, own, pltpu.roll(near, HEADDIM, axis=1))
    steps = None
    for index, piece in enumerate((own, near, far, across)):
        part = jnp.where((lanes >= HEADDIM) & (lanes < HEADDIM + heads), piece, 0.0)
        part = pltpu.roll(part, HEADDIM + 16 * index, axis=1)
        steps = part if steps is None else steps + part
    return both, steps


def small_gram_kernel(heads, own_ref, near_ref, far_ref, across_ref, gram_ref):
    blocks = small_blocks(own_ref[...], near_ref[...], far_ref[...], across_ref[...], heads)
    for index, block in enumerate(blocks):
        gram_ref[index] = gram3(block)


def small_apply_kernel(heads, own_ref, near_ref, far_ref, across_ref, factor_ref, weight_ref, out_ref):
    blocks = small_blocks(own_ref[...], near_ref[...], far_ref[...], across_ref[...], heads)
    both = product3(blocks[0], factor_ref[0])
    steps = pltpu.roll(product3(blocks[1], factor_ref[1]), HEADDIM, axis=1)
    ortho = jnp.where(lane_iota(both.shape) < HEADDIM, both, steps)
    weight = weight_ref[...]
    out_ref[...] = weight - muon_rate * (0.2 * math.sqrt(D) * ortho + decay_rate * weight)


def flipped(count, bits):
    return [(place, place ^ bits) for place in range(count)]


def ring_places(count):
    index = lax.axis_index("dp")
    if count != 8:
        return list(range(count)), index, lambda place: place
    here = jnp.where(lax.rem(index, 2) == 0, index // 2, 7 - index // 2)
    return [0, 2, 4, 6, 7, 5, 3, 1], here, lambda place: jnp.where(place < 4, 2 * place, 15 - 2 * place)


def place_kernel(count, halves, owner_ref, *refs):
    piece_refs, out_refs = refs[: count + halves], refs[count + halves :]
    for index in range(count):

        @pl.when(pl.program_id(0) == index)
        def _(index=index):
            piece = piece_refs[index][...]
            if halves and index == count - 1:
                piece = jnp.concatenate([piece, piece_refs[count][...]], axis=0)
            at = 0
            for out_ref in out_refs:
                width = out_ref.shape[1]
                out_ref[...] = piece[:, at : at + width]
                at += width


def ring_gather(shard, widths):
    count = lax.axis_size("dp")
    order, here, owner_at = ring_places(count)
    ahead = [(order[i], order[(i + 1) % count]) for i in range(count)]
    behind = [(b, a) for a, b in ahead]
    rows = shard.shape[0]
    halves = rows % 32 == 0
    pieces, distances = [shard], [0]
    forward = backward = shard
    for step in range(1, count // 2 + 1):
        last = step == count // 2
        if last and halves:
            forward, backward = forward[: rows // 2], backward[rows // 2 :]
        forward = lax.ppermute(forward, "dp", ahead)
        pieces.append(forward)
        distances.append(-step)
        if not last or halves:
            backward = lax.ppermute(backward, "dp", behind)
            pieces.append(backward)
            distances.append(step)
    if halves:
        distances.pop()
    owners = jnp.stack([owner_at(lax.rem(here + distance + count, count)) for distance in distances])
    return pl.pallas_call(
        functools.partial(place_kernel, count, int(halves)),
        grid_spec=pltpu.PrefetchScalarGridSpec(
            num_scalar_prefetch=1,
            grid=(count,),
            in_specs=[pl.BlockSpec(piece.shape, lambda i, owner_ref: (0, 0)) for piece in pieces],
            out_specs=[
                pl.BlockSpec((rows, width), lambda i, owner_ref: (owner_ref[i], 0))
                for width in widths
            ],
        ),
        out_shape=[jax.ShapeDtypeStruct((count * rows, width), shard.dtype) for width in widths],
        compiler_params=pltpu.CompilerParams(vmem_limit_bytes=24 * 2**20),
    )(owners.astype(jnp.int32), *pieces)


def scatter_near(left, rights, narrow):
    narrow = narrow and lax.axis_size("dp") == 8
    keep, send = run_grad(left, rights, narrow)
    return keep, lax.ppermute(send, "dp", flipped(lax.axis_size("dp"), 1))


def scatter_far(near, narrow):
    count = lax.axis_size("dp")
    parts = run_pair(*near, narrow and count == 8)
    return [parts[0]] + [
        lax.ppermute(part, "dp", flipped(count, 2 * distance))
        for distance, part in enumerate(parts)
        if distance
    ]


def reduce_all(value, axis):
    count = lax.axis_size(axis)
    bits = 1
    while bits < count:
        got = lax.ppermute(value, axis, flipped(count, bits))
        if bits * 2 == count:
            return value, got
        value = value + got
        bits *= 2


def reduce_mp(value):
    near, far, across = [lax.ppermute(value, "mp", flipped(4, bits)) for bits in (1, 2, 3)]
    return (value + near) + (far + across)


def gather_mp_stack(value):
    place = lax.axis_index("mp")
    out = jnp.zeros((4,) + value.shape, value.dtype)
    out = lax.dynamic_update_index_in_dim(out, value, place, 0)
    for bits in (1, 2, 3):
        got = lax.ppermute(value, "mp", flipped(4, bits))
        out = lax.dynamic_update_index_in_dim(out, got, place ^ bits, 0)
    return out


def mp_places():
    place = lax.axis_index("mp")
    return lax.rem(place, 2), place // 2


def own_rows(value):
    core, chip = mp_places()
    quarter = value.shape[0] // 4
    return lax.dynamic_slice_in_dim(value, (chip * 2 + core) * quarter, quarter, 0)


def assemble_kernel(count, adding, place_ref, *refs):
    add_ref, out_ref = refs[0], refs[-1]
    for index, piece_ref in enumerate(refs[adding : adding + count]):

        @pl.when(pl.program_id(0) == index)
        def _(piece_ref=piece_ref):
            if adding:
                out_ref[...] = add_ref[...].astype(f32) + piece_ref[...].astype(f32)
            else:
                out_ref[...] = piece_ref[...]


def assemble(pieces, places, add, total, before):
    rows = pieces[0].shape[0]
    piece = pl.BlockSpec((rows, D), lambda i, place_ref: (0, 0))
    whole = pl.BlockSpec((rows, D), lambda i, place_ref: (place_ref[i], 0))
    adds = [] if add is None else [add]
    befores = [] if before is None else [before]
    return pl.pallas_call(
        functools.partial(assemble_kernel, len(pieces), len(adds)),
        grid_spec=pltpu.PrefetchScalarGridSpec(
            num_scalar_prefetch=1,
            grid=(len(pieces),),
            in_specs=[whole] * len(adds)
            + [piece] * len(pieces)
            + [pl.BlockSpec(memory_space=pl.ANY)] * len(befores),
            out_specs=whole,
        ),
        out_shape=jax.ShapeDtypeStruct((total, D), bf16 if add is None else f32),
        input_output_aliases={1 + len(adds) + len(pieces): 0} if befores else {},
    )(places.astype(jnp.int32), *adds, *pieces, *befores)


def norm_back_kernel(place_ref, own_ref, got_ref, x_ref, gain_ref, out_ref, ggain_ref):
    x = x_ref[...].astype(f32)
    grad = own_ref[...] + got_ref[...].astype(f32)
    inv = lax.rsqrt(jnp.mean(x * x, axis=1, keepdims=True) + eps_norm)
    scaled = grad * gain_ref[...]
    pull = jnp.mean(x * scaled, axis=1, keepdims=True)
    out_ref[...] = (scaled * inv - x * (inv * inv * inv * pull)).astype(bf16)
    ggain_ref[...] = jnp.sum(grad * (x * inv), axis=0, keepdims=True)


def run_norm_back(part, own, got, block_in, gain, quarter):
    rows = got.shape[0]
    steps = own.shape[0] // rows
    gain_spec = pl.BlockSpec((1, D), lambda i, place_ref: (0, 0))
    return pl.pallas_call(
        norm_back_kernel,
        grid_spec=pltpu.PrefetchScalarGridSpec(
            num_scalar_prefetch=1,
            grid=(1,),
            in_specs=[
                pl.BlockSpec((rows, D), lambda i, place_ref: (part, 0)),
                pl.BlockSpec((rows, D), lambda i, place_ref: (0, 0)),
                pl.BlockSpec((rows, D), lambda i, place_ref: (place_ref[0] * steps + part, 0)),
                gain_spec,
            ],
            out_specs=[pl.BlockSpec((rows, D), lambda i, place_ref: (0, 0)), gain_spec],
        ),
        out_shape=[jax.ShapeDtypeStruct((rows, D), bf16), jax.ShapeDtypeStruct((1, D), f32)],
    )(quarter.reshape(1), own, got, block_in, gain)


def input_norm(features, gain_row):
    return (
        features
        * lax.rsqrt(jnp.mean(features * features, axis=1, keepdims=True) + eps_norm)
        * gain_row
    )


def adam_update(params_in, gradient, state_pair):
    moment_one = adam_first * state_pair[0] + (1.0 - adam_first) * gradient
    moment_two = adam_second * state_pair[1] + (1.0 - adam_second) * gradient * gradient
    scaled = (
        moment_one
        / (1.0 - adam_first**adam_steps)
        / (jnp.sqrt(moment_two / (1.0 - adam_second**adam_steps)) + 1e-08)
    )
    return (params_in - adam_rate * scaled, jnp.stack([moment_one, moment_two]))


def back_normed_kernel(sel_ref, a_ref, b_ref, small_ref, wz_ref, wx_ref, ws_ref, *refs):
    wa_ref, wb_ref = refs[-2:]
    half = wz_ref.shape[1] // 2
    step = pl.program_id(0)

    @pl.when(step == 0)
    def _():
        wa_ref[:, :half] = wz_ref[:, :half]
        wa_ref[:, half:] = wx_ref[:, :half]
        wb_ref[:, :half] = wz_ref[:, half:]
        wb_ref[:, half:] = wx_ref[:, half:]

    dims = (((0,), (1,)), ((), ()))
    total = (
        dot(a_ref[...], wa_ref[...], dims)
        + dot(b_ref[...], wb_ref[...], dims)
        + dot(small_ref[...], ws_ref[...], dims)
    )
    if len(refs) == 3:
        refs[0][...] = total
    else:
        got_ref, own_ref = refs[:2]
        total = total + got_ref[...]
        for index, send_ref in enumerate(refs[2:-2]):

            @pl.when(step == index)
            def _(send_ref=send_ref):
                send_ref[...] = total.astype(bf16)

        @pl.when(step >= len(refs) - 4)
        def _():
            own_ref[...] = total


def run_back_normed(core, chip, grads, weights, got):
    tok = grads[0].shape[1]
    block = SPAN
    steps = tok // 4 // block

    def grad_at(i, sel_ref):
        here = i // steps
        quarter = jnp.where(here == 0, 1 - sel_ref[1], sel_ref[1])
        return 0, (2 * quarter + sel_ref[0]) * steps + i % steps

    in_specs = [pl.BlockSpec((grad.shape[0], block), grad_at) for grad in grads]
    in_specs += [pl.BlockSpec(weight.shape, lambda i, sel_ref: (0, 0)) for weight in weights]
    arrays = [*grads, *weights]
    if got is None:
        out_specs = pl.BlockSpec((block, D), lambda i, sel_ref: (i, 0))
        out_shape = jax.ShapeDtypeStruct((2 * steps * block, D), f32)
    else:
        in_specs.append(pl.BlockSpec((block, D), lambda i, sel_ref: (i, 0)))
        arrays.append(got)
        out_specs = [pl.BlockSpec((block, D), lambda i, sel_ref: (jnp.maximum(i - steps, 0), 0))]
        out_specs += [pl.BlockSpec((block, D), lambda i, sel_ref: (0, 0))] * steps
        out_shape = [jax.ShapeDtypeStruct((steps * block, D), f32)]
        out_shape += [jax.ShapeDtypeStruct((block, D), bf16)] * steps
    return pl.pallas_call(
        back_normed_kernel,
        grid_spec=pltpu.PrefetchScalarGridSpec(
            num_scalar_prefetch=1,
            grid=(2 * steps,),
            in_specs=in_specs,
            out_specs=out_specs,
            scratch_shapes=[pltpu.VMEM(weights[0].shape, bf16)] * 2,
        ),
        out_shape=out_shape,
        compiler_params=pltpu.CompilerParams(vmem_limit_bytes=36 * 2**20),
    )(jnp.stack([core, chip]), *arrays)


def mm(left, right, left_dim, right_dim):
    return lax.dot_general(
        left, right, (((left_dim,), (right_dim,)), ((), ())), preferred_element_type=f32
    )


def tie(*values):
    return lax.optimization_barrier(values)


def step(
    block_in,
    cotangent,
    segment_ids,
    w_heads,
    w_bc,
    w_dt,
    mom_heads,
    mom_bc,
    mom_dt,
    norm_gain,
    inner_params,
    bc_params,
    head_params,
    norm_adam,
    inner_adam,
    bc_adam,
    head_adam,
):
    seq_here, length = segment_ids.shape
    tok_rows = seq_here * length
    rows_here, inner = w_heads.shape[1:]
    heads = head_params.shape[1]
    state_cols = w_bc.shape[1]
    step_row = state_cols
    pad_steps = jnp.zeros((rows_here, TILE - state_cols - heads), bf16)
    w_x_shard = jnp.concatenate(
        [w_heads[1].astype(bf16), w_bc.astype(bf16), w_dt.astype(bf16), pad_steps], axis=1
    )
    w_x, w_s = ring_gather(w_x_shard, (inner, TILE))
    w_oz_shard = jnp.concatenate([w_heads[2].astype(bf16), w_heads[0].astype(bf16)], axis=1)
    w_o, w_z = ring_gather(w_oz_shard, (inner, inner))
    normed = input_norm(block_in.astype(f32), norm_gain).astype(bf16)
    w_heads, mom_heads, w_bc, w_dt, mom_bc, mom_dt, norm_adam, inner_adam, bc_adam, head_adam, w_s = tie(
        w_heads, mom_heads, w_bc, w_dt, mom_bc, mom_dt, norm_adam, inner_adam, bc_adam, head_adam, w_s
    )
    core, chip = mp_places()
    seg = segment_ids[:, None]
    taps = jnp.pad(inner_params.T, ((0, 0), (0, 2)))
    state_taps = jnp.pad(bc_params.T, ((0, 0), (0, 3)))
    headcol = jnp.pad(head_params.T, ((0, 16 - heads), (0, TILE - 3)))

    small = mm(w_s, normed, 0, 1)
    state_own = run_state_forward(small, 0, seg, state_taps)
    bc = gather_mp_stack(state_own).reshape(4 * state_cols, tok_rows)
    raw = mm(w_x, normed, 0, 1)
    done = None
    for first, count in ((0, 1), (1, seq_here - 2), (seq_here - 1, 1)):
        done = run_forward(
            first, count, done, raw, small, step_row, bc, seg, taps, headcol, head_params
        )
    y, state = done
    d_o = mm(w_o, cotangent, 0, 1)
    z = mm(w_z, normed, 0, 1)
    sums = run_gate_sums(y, z, d_o, taps)
    sums = reduce_mp(sums)
    sums, w_o_swap = tie(sums, w_o)
    w_o_far = lax.ppermute(w_o_swap, "mp", flipped(4, 2))
    inv = lax.rsqrt(sums[0] / INNER + eps_norm)
    pull = inv * inv * inv * sums[1] / INNER
    norm_rows = jnp.stack([inv.reshape(seq_here, length), pull.reshape(seq_here, length)], axis=1)
    out_bf, out_send = run_gate_out(y, z, inv[None], taps, chip)
    out_far = lax.ppermute(out_send, "mp", flipped(4, 2))
    o_near = scatter_near(cotangent, [(out_bf, inner, 0)], True)

    def backward(part, raw):
        return run_backward(
            part, 2, raw, z, y, d_o, small, step_row, bc, seg, norm_rows, state, taps, headcol, head_params
        )

    d_zx_a, d_step_a, d_bc_a, g_conv_a, g_head_a = backward(0, raw)
    d_zx_a, raw = tie(d_zx_a, raw)
    d_zx_b, d_step_b, d_bc_b, g_conv_b, g_head_b = backward(1, raw)
    a_near = scatter_near(normed, [(d_zx_a, inner, 0)], False)
    o_parts = scatter_far(o_near, False)
    a_parts = scatter_far(a_near, True)

    w_heads, mom_heads, d_zx_b, out_bf, block_late, cot_late = tie(
        w_heads, mom_heads, d_zx_b, out_bf, block_in, cotangent
    )
    half_tok = tok_rows // 2
    out_keep = lax.dynamic_slice_in_dim(out_bf, chip * half_tok, half_tok, 1)
    branch = mm(out_keep, w_o, 0, 1) + mm(out_far, w_o_far, 0, 1)
    branch = branch.reshape(2, half_tok // 2, D)
    send = lax.dynamic_index_in_dim(branch, 1 - core, 0, keepdims=False)
    keep = lax.dynamic_index_in_dim(branch, core, 0, keepdims=False)
    branch_own = keep + lax.ppermute(send, "mp", flipped(4, 1))
    block_own = (own_rows(block_late).astype(f32) + branch_own).astype(bf16)
    out_x = lax.ppermute(block_own, "mp", flipped(4, 2))
    out_core = lax.ppermute(block_own, "mp", flipped(4, 1))
    out_last = lax.ppermute(out_x, "mp", flipped(4, 1))
    places = jnp.stack([chip * 2 + core, chip * 2 + 1 - core, 2 - chip * 2 + core, 3 - chip * 2 - core])
    block_out = assemble([block_own, out_core, out_x, out_last], places, None, tok_rows, None)

    d_bc = (d_bc_a + d_bc_b).reshape(2, 2, state_cols, tok_rows)
    send = lax.dynamic_index_in_dim(d_bc, 1 - core, 1, keepdims=False)
    keep = lax.dynamic_index_in_dim(d_bc, core, 1, keepdims=False)
    d_bc = keep + lax.ppermute(send, "mp", flipped(4, 1))
    send = lax.dynamic_index_in_dim(d_bc, 1 - chip, 0, keepdims=False)
    keep = lax.dynamic_index_in_dim(d_bc, chip, 0, keepdims=False)
    d_state = keep + lax.ppermute(send, "mp", flipped(4, 2))
    d_raw, g_state = run_state_backward(small, 0, d_state, seg, state_taps)
    d_small = jnp.concatenate(
        [
            d_raw,
            d_step_a[: heads // 2],
            d_step_b[heads // 2 : heads],
            jnp.zeros((TILE - state_cols - heads, tok_rows), bf16),
        ],
        axis=0,
    )
    half_in = inner // 2
    c_near = scatter_near(normed, [(d_zx_b, half_in, 0)], True)
    d_near = scatter_near(normed, [(d_zx_b, half_in, 1), (d_small, TILE, 0)], False)
    c_parts = scatter_far(c_near, False)
    d_parts = scatter_far(d_near, True)

    back = (d_zx_a, d_zx_b, d_small), (w_z, w_x, w_s)
    send = run_back_normed(1 - core, chip, *back, None)
    got = lax.ppermute(send, "mp", flipped(4, 1))
    normed_own, *sends = run_back_normed(core, chip, *back, got)
    pieces = ([], [], [], [])
    gains = []
    for part, send in enumerate(sends):
        got = lax.ppermute(send, "mp", flipped(4, 2))
        back_x, gain = run_norm_back(
            part, normed_own, got, block_late, norm_gain[None], chip * 2 + core
        )
        gains.append(gain)
        far = lax.ppermute(back_x, "mp", flipped(4, 2))
        pieces[0].append(back_x)
        pieces[1].append(lax.ppermute(back_x, "mp", flipped(4, 1)))
        pieces[2].append(far)
        pieces[3].append(lax.ppermute(far, "mp", flipped(4, 1)))
    places = (places[:, None] * len(sends) + jnp.arange(len(sends))).reshape(-1)
    near_count = 2 * len(sends)
    grad_block = assemble(pieces[0] + pieces[1], places[:near_count], cot_late, tok_rows, None)
    grad_block = assemble(
        pieces[2] + pieces[3], places[near_count:], cot_late, tok_rows, grad_block
    )
    gain = sum(gains[1:], gains[0]).reshape(-1, TILE)
    gain = reduce_mp(gain)

    spots = (
        (4, lambda i: (jnp.where(i < 2, 2, i - 2), 0, jnp.where(i < 2, i, 0))),
        (2, lambda i: (i, 0, 1)),
    )
    pad_small = jnp.zeros((rows_here, TILE - state_cols - heads), f32)
    small_mom = jnp.concatenate([mom_bc, mom_dt, pad_small], axis=1)
    small_weight = jnp.concatenate([w_bc, w_dt, pad_small], axis=1)
    *stacks, gram_a = run_momentum((o_parts, a_parts), mom_heads, spots[0], None, None)
    grad_heads, new_mom_heads, gram_d, grad_small, new_small = run_momentum(
        (c_parts, d_parts), mom_heads, spots[1], stacks, small_mom
    )
    new_w_heads = None
    for gram, spot in ((gram_a, spots[0]), (gram_d, spots[1])):
        gram = reduce_all(gram, "dp")
        factor = run_factor(*gram, head_factor_kernel)
        new_w_heads = run_apply(w_heads, new_mom_heads, factor, spot, new_w_heads)
    grad_bc = grad_small[:, :state_cols]
    grad_dt = grad_small[:, state_cols : state_cols + heads]
    new_mom_bc = new_small[:, :state_cols]
    new_mom_dt = new_small[:, state_cols : state_cols + heads]
    columns = [new_small]
    for bits in (1, 2, 3):
        columns.append(lax.ppermute(new_small, "mp", flipped(4, bits)))
    gram = pl.pallas_call(
        functools.partial(small_gram_kernel, heads),
        out_shape=jax.ShapeDtypeStruct((2, TILE, TILE), f32),
    )(*columns)

    g_head = g_head_a + g_head_b
    vectors = [
        jnp.concatenate([g_conv_a, g_conv_b], axis=0),
        jnp.sum(g_state, axis=-1),
        jnp.sum(g_head, axis=-1),
        gain,
    ]
    flat = jnp.concatenate([part.reshape(-1) for part in vectors])
    sized = -(-flat.shape[0] // (8 * TILE)) * 8 * TILE
    flat = jnp.pad(flat, (0, sized - flat.shape[0])).reshape(-1, TILE)
    flat = jnp.concatenate([gram.reshape(-1, TILE), flat], axis=0)
    flat = reduce_all(flat, "dp")
    split_at = 2 * TILE
    grams = [part[:split_at].reshape(2, TILE, TILE) for part in flat]
    flat = (flat[0][split_at:] + flat[1][split_at:]).reshape(-1)
    parts = []
    at = 0
    for part in vectors:
        parts.append(flat[at : at + part.size].reshape(part.shape))
        at += part.size
    grad_inner = parts[0].T[: CONV + 2]
    grad_bc_params = parts[1]
    grad_head_params = parts[2][:, :heads]
    grad_norm_gain = parts[3].reshape(-1)
    factor = run_factor(*grams, full_factor_kernel)
    new_weight = pl.pallas_call(
        functools.partial(small_apply_kernel, heads),
        out_shape=jax.ShapeDtypeStruct((rows_here, TILE), f32),
    )(*columns, factor, small_weight)
    new_w_bc = new_weight[:, :state_cols]
    new_w_dt = new_weight[:, state_cols : state_cols + heads]
    new_norm_gain, new_norm_adam = adam_update(norm_gain, grad_norm_gain, norm_adam)
    new_inner_params, new_inner_adam = adam_update(inner_params, grad_inner, inner_adam)
    new_bc_params, new_bc_adam = adam_update(bc_params, grad_bc_params, bc_adam)
    new_head_params, new_head_adam = adam_update(head_params, grad_head_params, head_adam)
    return (
        block_out,
        grad_block,
        grad_heads,
        grad_bc,
        grad_dt,
        grad_norm_gain,
        grad_inner,
        grad_bc_params,
        grad_head_params,
        new_w_heads,
        new_w_bc,
        new_w_dt,
        new_mom_heads,
        new_mom_bc,
        new_mom_dt,
        new_norm_gain,
        new_inner_params,
        new_bc_params,
        new_head_params,
        new_norm_adam,
        new_inner_adam,
        new_bc_adam,
        new_head_adam,
    )


def solution(mesh):
    in_specs = (
        P("dp", None),
        P("dp", None),
        P("dp", None),
        P(None, "dp", "mp"),
        P("dp", "mp"),
        P("dp", "mp"),
        P(None, "dp", "mp"),
        P("dp", "mp"),
        P("dp", "mp"),
        P(),
        P(None, "mp"),
        P(None, "mp"),
        P(None, "mp"),
        P(),
        P(None, None, "mp"),
        P(None, None, "mp"),
        P(None, None, "mp"),
    )
    out_specs = (
        P("dp", None),
        P("dp", None),
        P(None, "dp", "mp"),
        P("dp", "mp"),
        P("dp", "mp"),
        P(),
        P(None, "mp"),
        P(None, "mp"),
        P(None, "mp"),
        P(None, "dp", "mp"),
        P("dp", "mp"),
        P("dp", "mp"),
        P(None, "dp", "mp"),
        P("dp", "mp"),
        P("dp", "mp"),
        P(),
        P(None, "mp"),
        P(None, "mp"),
        P(None, "mp"),
        P(),
        P(None, None, "mp"),
        P(None, None, "mp"),
        P(None, None, "mp"),
    )
    return jax.shard_map(step, mesh=mesh, in_specs=in_specs, out_specs=out_specs, check_vma=False)
```

time: 2330 us -> 772 us (0.33)
  waiting for transfers between devices: 1160 us -> 254 us
  matrix products: 400 us -> 39.1 us
  Pallas kernels: 0 us -> 246 us
  other arithmetic: 292 us -> 51 us
  local copies, waits for them, and re-layouts: 300 us -> 89.8 us
  blocking collectives: 124 us -> 0 us
  starting transfers between devices: 8.39 us -> 78.4 us
    psum x6 -> x0, waiting for transfers between devices: 716 us -> none  [the longest x1 422 us: body(): branch_sum = lax.psum(branch_part, 'mp')]
    dot_general x111 -> x6, matrix products: 369 us -> 39.1 us  [mm(): lax.dot_general(left, right, (((left_dim,), (right_dim,)), ((), ())), pre...]
    ppermute x0 -> x70, waiting for transfers between devices: none -> 254 us  [the longest x4 71.8 us: scatter_near(): return (keep, lax.ppermute(send, 'dp', flipped(lax.axis_size('dp'), 1)))]
    pallas_call x0 -> x35, Pallas kernels: none -> 246 us  [the longest x2 55.5 us: run_backward(): pl.pallas_call(functools.partial(backward_kernel, part * heads, heads), g...]
    reduce_scatter x1 -> x0, waiting for transfers between devices: 207 us -> none  [body(): lax.psum_scatter(jnp.stack([grad_zed, grad_xin, grad_wout]), 'dp', scatte...]
    unnamed x15 -> x0, waiting for transfers between devices: 132 us -> none
    all_gather x2 -> x0, waiting for transfers between devices: 86.8 us -> none  [the longest x1 86.8 us: body(): lax.all_gather(w_heads.astype(jnp.bfloat16), 'dp', axis=1, tiled=True)]
    ppermute x0 -> x70, starting transfers between devices: none -> 78.4 us  [the longest x12 26.4 us: scatter_far(): lax.ppermute(part, 'dp', flipped(count, 2 * distance))]
  transfers between devices with their start and end apart: 14 -> 70, of which waited for: 12 -> 24; matrix products, arithmetic and copies ran while one was open for 8% -> 15% of each run, Pallas kernels for 0% -> 22%
where the time goes in v1:
time: 772 us; the launch traced here: 761 us
  waiting for transfers between devices  254 us (33%)
  Pallas kernels  246 us (32%)
  local copies, waits for them, and re-layouts  89.8 us (12%)
  starting transfers between devices  78.4 us (10%)
  other arithmetic  51 us (7%)
  matrix products  39.1 us (5%)
    ppermute x4, waiting for transfers between devices, scatter_near(): return (keep, lax.ppermute(send, 'dp', flipped(lax.axis_size('dp'), 1)))  71.8 us
    unnamed x227, local copies, waits for them, and re-layouts  57.7 us
    pallas_call x2, Pallas kernels, run_backward(): pl.pallas_call(functools.partial(backward_kernel, part * heads, heads), g...  55.5 us
    ppermute x12, waiting for transfers between devices, scatter_far(): lax.ppermute(part, 'dp', flipped(count, 2 * distance))  53.3 us
    ppermute x1, waiting for transfers between devices, step(): d_state = keep + lax.ppermute(send, 'mp', flipped(4, 2))  47.3 us
    dot_general x6, matrix products, mm(): lax.dot_general(left, right, (((left_dim,), (right_dim,)), ((), ())), pre...  39.1 us
    pallas_call x4, Pallas kernels, run_grad(): pl.pallas_call(grad_kernel, grid_spec=pltpu.PrefetchScalarGridSpec(num_sc...  31.7 us
    ppermute x8, waiting for transfers between devices, ring_gather(): forward = lax.ppermute(forward, 'dp', ahead)  29.5 us
  transfers between devices with their start and end apart: 70, of which 24 were waited for; matrix products, arithmetic and copies ran while one was open for 15% of the time, Pallas kernels for 22%

profile of v1, /device:TPU:0, one launch (start us, length us, event | category | flops | bytes accessed | tf_op | source)
XLA Modules:
  0.0 761.0 jit_solution(7927137911884519335)
XLA Ops:
  6.4 8.0 %collective-permute-done.refs_1_ = bf16[192,896]{1,0:T(8,128)(2,1)S(1)} collective-permute-done((bf16[192,896]{1,0:T(8,128)(2,1)S(1)}, bf16[192,896]{1,0:T(8,128)(2,1)S(1)}, u32[]{:S(2)}, u32[]{:S(2)}) %collective-permute-start) | collective-permute-done | bytes 344096 | tf_op jit(solution)/shard_map/ppermute | solution.py:904
  18.5 6.8 collective-permute-done.2.refs_3_
  31.5 6.4 collective-permute-done.8.refs_1_
  82.9 8.0 %fusion.29.refs_0_.raw_ref = f32[768,2048]{1,0:T(8,128)S(1)} fusion(bf16[1536,768]{1,0:T(8,128)(2,1)} %copy-done.17, bf16[2048,1536]{1,0:T(8,128)(2,1)} %fusion.2.left_ref), kind=kOutput, calls=%fused_computation.89 | convolution fusion | flops 4831838208 | bytes 14942208 | tf_op jit(solution)/shard_map/dot_general | solution.py:1138
  96.4 6.5 shard_map.347
  103.0 11.6 %shard_map.348 = (f32[768,2048]{1,0:T(8,128)S(1)}, f32[4,768,128]{2,1,0:T(8,128)S(1)}) custom-call(f32[768,2048]{1,0:T(8,128)S(1)} %fusion.29.refs_0_.raw_ref, f32[128,2048]{1,0:T(8,128)S(1)} %copy-done.5, bf16[256,2048]{1,0:T(8,128)(2,1)S(1)} %bitcast.146, s32[4,1,512]{2,1,0:T(1,128)S(1)} %copy-done.33, ...), custom_call_target="tpu_custom_call", output_to_operand_aliasing={{0}: (7, {}), {1}: (8, {})} | custom-call | tf_op jit(solution)/shard_map/pallas_call | solution.py:386
  121.9 8.2 %shard_map.345 = (bf16[1536,768]{1,0:T(8,128)(2,1)}, bf16[1536,768]{1,0:T(8,128)(2,1)S(1)}) custom-call(s32[8]{0:T(128)S(1)} %stack.117.owner_ref, bf16[192,1536]{1,0:T(8,128)(2,1)S(1)} %pad_maximum_fusion.refs_0_, bf16[192,1536]{1,0:T(8,128)(2,1)S(1)} %copy-done.32, bf16[192,1536]{1,0:T(8,128)(2,1)} %collective-permute-done.9.refs_2_, ...), custom_call_target="tpu_custom_call" | custom-call | tf_op jit(solution)/shard_map/pallas_call | solution.py:914
  130.1 7.0 fusion.30.z_ref
  137.1 8.7 %fusion.32.do_ref = f32[768,2048]{1,0:T(8,128)} fusion(bf16[1536,768]{1,0:T(8,128)(2,1)} %get-tuple-element.128, bf16[2048,1536]{1,0:T(8,128)(2,1)S(1)} %bitcast.142), kind=kOutput, calls=%fused_computation.92 | convolution fusion | flops 4831838208 | bytes 14942208 | tf_op jit(solution)/shard_map/dot_general | solution.py:1138
  145.8 8.9 %shard_map.350 = f32[2,2048]{1,0:T(2,128)} custom-call(f32[768,2048]{1,0:T(8,128)} %copy-done, f32[768,2048]{1,0:T(8,128)} %fusion.30.z_ref, f32[768,2048]{1,0:T(8,128)} %fusion.32.do_ref, f32[768,8]{1,0:T(8,128)} %copy-done.12), custom_call_target="tpu_custom_call" | custom-call | tf_op jit(solution)/shard_map/pallas_call | solution.py:459
  168.7 27.7 %shard_map.351 = (bf16[768,2048]{1,0:T(8,128)(2,1)S(1)}, bf16[16,2048]{1,0:T(8,128)(2,1)S(1)}, f32[256,2048]{1,0:T(8,128)S(1)}, f32[384,8]{1,0:T(8,128)S(1)}, f32[3,16,128]{2,1,0:T(8,128)S(1)}) custom-call(f32[768,2048]{1,0:T(8,128)S(1)} %copy-done.3, f32[768,2048]{1,0:T(8,128)S(1)} %copy-done.4, f32[768,2048]{1,0:T(8,128)} %copy-done, ...), custom_call_target="tpu_custom_call" | custom-call | tf_op jit(solution)/shard_map/pallas_call | solution.py:433
  198.7 27.8 %shard_map.352 = (bf16[768,2048]{1,0:T(8,128)(2,1)S(1)}, bf16[16,2048]{1,0:T(8,128)(2,1)S(1)}, f32[256,2048]{1,0:T(8,128)S(1)}, f32[384,8]{1,0:T(8,128)S(1)}, f32[3,16,128]{2,1,0:T(8,128)S(1)}) custom-call(f32[768,2048]{1,0:T(8,128)S(1)} %copy-done.3, f32[768,2048]{1,0:T(8,128)S(1)} %copy-done.4, f32[768,2048]{1,0:T(8,128)} %copy-done, ...), custom_call_target="tpu_custom_call" | custom-call | tf_op jit(solution)/shard_map/pallas_call | solution.py:433
  234.2 8.4 %shard_map.353 = (bf16[768,2048]{1,0:T(8,128)(2,1)}, bf16[768,1024]{1,0:T(8,128)(2,1)}) custom-call(s32[1]{0:T(128)} %bitcast.26.chip_ref, f32[768,2048]{1,0:T(8,128)} %copy-done, f32[768,2048]{1,0:T(8,128)} %fusion.30.z_ref, f32[1,2048]{1,0:T(1,128)} %copy-done.83, f32[768,8]{1,0:T(8,128)} %copy-done.12), custom_call_target="tpu_custom_call" | custom-call | tf_op jit(solution)/shard_map/pallas_call | solution.py:489
  247.0 47.3 %collective-permute-done.29 = f32[64,2048]{1,0:T(8,128)} collective-permute-done((f32[64,2048]{1,0:T(8,128)}, f32[64,2048]{1,0:T(8,128)}, u32[]{:S(2)}, u32[]{:S(2)}) %collective-permute-start.29) | collective-permute-done | bytes 524320 | tf_op jit(solution)/shard_map/ppermute | solution.py:1247
  306.9 9.7 %shard_map.356 = f32[1024,1536]{1,0:T(8,128)} custom-call(s32[2]{0:T(128)S(1)} %pad_add_fusion.2.sel_ref, bf16[768,2048]{1,0:T(8,128)(2,1)S(1)} %copy-done.9, bf16[768,2048]{1,0:T(8,128)(2,1)S(1)} %copy-done.7, bf16[128,2048]{1,0:T(8,128)(2,1)S(1)} %maximum_maximum_fusion.small_ref.refs_1_, bf16[1536,768]{1,0:T(8,128)(2,1)S(1)} %copy-done.21, ...), custom_call_target="tpu_custom_call" | custom-call | tf_op jit(solution)/shard_map/pallas_call | solution.py:1123
  316.7 10.6 %collective-permute-done.22 = bf16[768,1024]{1,0:T(8,128)(2,1)} collective-permute-done((bf16[768,1024]{1,0:T(8,128)(2,1)}, bf16[768,1024]{1,0:T(8,128)(2,1)}, u32[]{:S(2)}, u32[]{:S(2)}) %collective-permute-start.22) | collective-permute-done | bytes 1572896 | tf_op jit(solution)/shard_map/ppermute | solution.py:1209
  341.5 9.5 %shard_map.366 = (f32[4,192,768]{2,1,0:T(8,128)S(1)}, bf16[4,192,768]{2,1,0:T(8,128)(2,1)}) custom-call(s32[1]{0:T(128)} %bitcast.38.place_ref, bf16[2048,1536]{1,0:T(8,128)(2,1)S(1)} %bitcast.144, bf16[768,2048]{1,0:T(8,128)(2,1)S(1)} %copy-done.26), custom_call_target="tpu_custom_call" | custom-call | tf_op jit(solution)/shard_map/pallas_call | solution.py:632
  351.7 9.7 %shard_map.368 = (f32[4,192,768]{2,1,0:T(8,128)S(1)}, f32[4,192,768]{2,1,0:T(8,128)}) custom-call(s32[1]{0:T(128)} %bitcast.38.place_ref, bf16[2048,1536]{1,0:T(8,128)(2,1)S(1)} %bitcast.140, bf16[768,2048]{1,0:T(8,128)(2,1)S(1)} %copy-done.10), custom_call_target="tpu_custom_call" | custom-call | tf_op jit(solution)/shard_map/pallas_call | solution.py:632
  371.1 71.8 %collective-permute-done.39.got_ref = bf16[4,192,384]{2,1,0:T(8,128)(2,1)S(1)} collective-permute-done((bf16[4,192,384]{2,1,0:T(8,128)(2,1)S(1)}, bf16[4,192,384]{2,1,0:T(8,128)(2,1)S(1)}, u32[]{:S(2)}, u32[]{:S(2)}) %collective-permute-start.39) | collective-permute-done | bytes 589856 | tf_op jit(solution)/shard_map/ppermute | solution.py:933
  455.4 6.7 collective-permute-done.40.refs_1_
  470.8 7.2 shard_map.364
  496.1 26.4 %collective-permute-done.49.refs_2_ = f32[192,768]{1,0:T(8,128)} collective-permute-done((f32[192,768]{1,0:T(8,128)}, f32[192,768]{1,0:T(8,128)}, u32[]{:S(2)}, u32[]{:S(2)}) %collective-permute-start.49) | collective-permute-done | bytes 589856 | tf_op jit(solution)/shard_map/ppermute | solution.py:940
  522.5 14.3 %collective-permute-start.53 = (bf16[192,768]{1,0:T(8,128)(2,1)}, bf16[192,768]{1,0:T(8,128)(2,1)S(1)}, u32[]{:S(2)}, u32[]{:S(2)}) collective-permute-start(bf16[192,768]{1,0:T(8,128)(2,1)} %get-tuple-element.167), channel_id=1, source_target_pairs={{0,16},{4,20},{8,24},{12,28},{16,0},{20,4},{24,8},{28,12},{1,17},{... | collective-permute-start | bytes 884744 | tf_op jit(solution)/shard_map/ppermute | solution.py:940
  544.3 10.9 %shard_map.357 = (f32[512,1536]{1,0:T(8,128)S(1)}, bf16[256,1536]{1,0:T(8,128)(2,1)}, bf16[256,1536]{1,0:T(8,128)(2,1)}) custom-call(s32[2]{0:T(128)S(1)} %pad_add_fusion.1.sel_ref, bf16[768,2048]{1,0:T(8,128)(2,1)S(1)} %copy-done.11, bf16[768,2048]{1,0:T(8,128)(2,1)S(1)} %copy-done.7, bf16[128,2048]{1,0:T(8,128)(2,1)S(1)} %copy-done.25, ...), custom_call_target="tpu_custom_call" | custom-call | tf_op jit(solution)/shard_map/pallas_call | solution.py:1123
  566.0 12.8 %collective-permute-done.45.refs_6_.refs_11_ = bf16[192,512]{1,0:T(8,128)(2,1)S(1)} collective-permute-done((bf16[192,512]{1,0:T(8,128)(2,1)}, bf16[192,512]{1,0:T(8,128)(2,1)S(1)}, u32[]{:S(2)}, u32[]{:S(2)}) %collective-permute-start.45) | collective-permute-done | bytes 196640 | tf_op jit(solution)/shard_map/ppermute | solution.py:940
  638.0 6.8 collective-permute-done.65
  664.7 7.7 %shard_map.374.factor_ref = f32[12,128,128]{2,1,0:T(8,128)} custom-call(f32[12,64,128]{2,1,0:T(8,128)} %add.322.gram_ref, f32[12,64,128]{2,1,0:T(8,128)} %collective-permute-done.69.got_ref), custom_call_target="tpu_custom_call" | custom-call | tf_op jit(solution)/shard_map/pallas_call | solution.py:807
  685.7 6.7 shard_map.354
  705.5 7.5 collective-permute-done.34.refs_2_
  713.0 16.4 %collective-permute-done.32.refs_1_ = bf16[256,1536]{1,0:T(8,128)(2,1)S(1)} collective-permute-done((bf16[256,1536]{1,0:T(8,128)(2,1)}, bf16[256,1536]{1,0:T(8,128)(2,1)S(1)}, u32[]{:S(2)}, u32[]{:S(2)}) %collective-permute-start.32) | collective-permute-done | bytes 786464 | tf_op jit(solution)/shard_map/ppermute | solution.py:1276
  747.0 6.8 shard_map.360.refs_5_
  753.9 6.8 shard_map.361
  (490 shorter events, 319.3 us)
Async XLA Ops:
  58.0 33.1 %collective-permute-start.12 = (bf16[192,1536]{1,0:T(8,128)(2,1)}, bf16[192,1536]{1,0:T(8,128)(2,1)}, u32[]{:S(2)}, u32[]{:S(2)}) collective-permute-start(bf16[192,1536]{1,0:T(8,128)(2,1)} %collective-permute-done.10.refs_3_), channel_id=1, source_target_pairs={{0,8},{8,16},{16,24},{24,28},{28,20},{20,12},{12,4},{4,0},{1,9},{9... | collective-permute-start | bytes 1769480 | tf_op jit(solution)/shard_map/ppermute | solution.py:904
  59.8 35.1 %collective-permute-start.13 = (bf16[192,1536]{1,0:T(8,128)(2,1)}, bf16[192,1536]{1,0:T(8,128)(2,1)}, u32[]{:S(2)}, u32[]{:S(2)}) collective-permute-start(bf16[192,1536]{1,0:T(8,128)(2,1)} %collective-permute-done.11.refs_4_), channel_id=1, source_target_pairs={{8,0},{16,8},{24,16},{28,24},{20,28},{12,20},{4,12},{0,4},{9,1},{1... | collective-permute-start | bytes 1769480 | tf_op jit(solution)/shard_map/ppermute | solution.py:908
  93.3 28.6 %collective-permute-start.14 = (bf16[96,1536]{1,0:T(8,128)(2,1)S(1)}, bf16[96,1536]{1,0:T(8,128)(2,1)S(1)}, u32[]{:S(2)}, u32[]{:S(2)}) collective-permute-start(bf16[96,1536]{1,0:T(8,128)(2,1)S(1)} %slice.171), channel_id=1, source_target_pairs={{0,8},{8,16},{16,24},{24,28},{28,20},{20,12},{12,4},{4,0},{1,9},{9... | collective-permute-start | bytes 884744 | tf_op jit(solution)/shard_map/ppermute | solution.py:904
  95.9 26.0 %collective-permute-start.15 = (bf16[96,1536]{1,0:T(8,128)(2,1)S(1)}, bf16[96,1536]{1,0:T(8,128)(2,1)S(1)}, u32[]{:S(2)}, u32[]{:S(2)}) collective-permute-start(bf16[96,1536]{1,0:T(8,128)(2,1)S(1)} %slice.172), channel_id=1, source_target_pairs={{8,0},{16,8},{24,16},{28,24},{20,28},{12,20},{4,12},{0,4},{9,1},{1... | collective-permute-start | bytes 884744 | tf_op jit(solution)/shard_map/ppermute | solution.py:908
  228.6 98.8 %collective-permute-start.23 = (bf16[1536,768]{1,0:T(8,128)(2,1)}, bf16[1536,768]{1,0:T(8,128)(2,1)}, u32[]{:S(2)}, u32[]{:S(2)}) collective-permute-start(bf16[1536,768]{1,0:T(8,128)(2,1)} %get-tuple-element.128), channel_id=1, source_target_pairs={{0,2},{1,3},{2,0},{3,1},{4,6},{5,7},{6,4},{7,5},{8,10},{9,11},{10,... | collective-permute-start | bytes 7077896 | tf_op jit(solution)/shard_map/ppermute | solution.py:1204
  233.5 60.8 %collective-permute-start.29 = (f32[64,2048]{1,0:T(8,128)}, f32[64,2048]{1,0:T(8,128)}, u32[]{:S(2)}, u32[]{:S(2)}) collective-permute-start(f32[64,2048]{1,0:T(8,128)} %dynamic-slice_bitcast_fusion.2), channel_id=1, source_target_pairs={{0,2},{1,3},{2,0},{3,1},{4,6},{5,7},{6,4},{7,5},{8,10},{9,11},{10,... | collective-permute-start | bytes 1572872 | tf_op jit(solution)/shard_map/ppermute | solution.py:1247
  242.7 84.7 %collective-permute-start.22 = (bf16[768,1024]{1,0:T(8,128)(2,1)}, bf16[768,1024]{1,0:T(8,128)(2,1)}, u32[]{:S(2)}, u32[]{:S(2)}) collective-permute-start(bf16[768,1024]{1,0:T(8,128)(2,1)} %get-tuple-element.127), channel_id=1, source_target_pairs={{0,2},{1,3},{2,0},{3,1},{4,6},{5,7},{6,4},{7,5},{8,10},{9,11},{10,... | collective-permute-start | bytes 4718600 | tf_op jit(solution)/shard_map/ppermute | solution.py:1209
  316.6 220.2 %collective-permute-start.30 = (f32[1024,1536]{1,0:T(8,128)}, f32[1024,1536]{1,0:T(8,128)}, u32[]{:S(2)}, u32[]{:S(2)}) collective-permute-start(f32[1024,1536]{1,0:T(8,128)} %shard_map.356), channel_id=1, source_target_pairs={{0,1},{1,0},{2,3},{3,2},{4,5},{5,4},{6,7},{7,6},{8,9},{9,8},{10,11... | collective-permute-start | bytes 18874376 | tf_op jit(solution)/shard_map/ppermute | solution.py:1266
  341.5 142.8 %collective-permute-start.24 = (f32[512,1536]{1,0:T(8,128)}, f32[512,1536]{1,0:T(8,128)}, u32[]{:S(2)}, u32[]{:S(2)}) collective-permute-start(f32[512,1536]{1,0:T(8,128)} %dynamic-slice_bitcast_fusion), channel_id=1, source_target_pairs={{0,1},{1,0},{2,3},{3,2},{4,5},{5,4},{6,7},{7,6},{8,9},{9,8},{10,11... | collective-permute-start | bytes 9437192 | tf_op jit(solution)/shard_map/ppermute | solution.py:1233
  351.1 97.5 %collective-permute-start.47 = (bf16[4,192,768]{2,1,0:T(8,128)(2,1)}, bf16[4,192,768]{2,1,0:T(8,128)(2,1)}, u32[]{:S(2)}, u32[]{:S(2)}) collective-permute-start(bf16[4,192,768]{2,1,0:T(8,128)(2,1)} %get-tuple-element.158), channel_id=1, source_target_pairs={{0,4},{4,0},{8,12},{12,8},{16,20},{20,16},{24,28},{28,24},{1,5},{5... | collective-permute-start | bytes 3538952 | tf_op jit(solution)/shard_map/ppermute | solution.py:933
  362.7 128.4 %collective-permute-start.51 = (f32[4,192,768]{2,1,0:T(8,128)}, f32[4,192,768]{2,1,0:T(8,128)}, u32[]{:S(2)}, u32[]{:S(2)}) collective-permute-start(f32[4,192,768]{2,1,0:T(8,128)} %get-tuple-element.164), channel_id=1, source_target_pairs={{0,4},{4,0},{8,12},{12,8},{16,20},{20,16},{24,28},{28,24},{1,5},{5... | collective-permute-start | bytes 7077896 | tf_op jit(solution)/shard_map/ppermute | solution.py:933
  370.5 72.4 %collective-permute-start.39 = (bf16[4,192,384]{2,1,0:T(8,128)(2,1)S(1)}, bf16[4,192,384]{2,1,0:T(8,128)(2,1)S(1)}, u32[]{:S(2)}, u32[]{:S(2)}) collective-permute-start(bf16[4,192,384]{2,1,0:T(8,128)(2,1)S(1)} %get-tuple-element.143), channel_id=1, source_target_pairs={{0,4},{4,0},{8,12},{12,8},{16,20},{20,16},{24,28},{28,24},{1,5},{5... | collective-permute-start | bytes 1769480 | tf_op jit(solution)/shard_map/ppermute | solution.py:933
  483.5 74.7 %collective-permute-start.43 = (f32[4,192,512]{2,1,0:T(8,128)}, f32[4,192,512]{2,1,0:T(8,128)}, u32[]{:S(2)}, u32[]{:S(2)}) collective-permute-start(f32[4,192,512]{2,1,0:T(8,128)} %get-tuple-element.149), channel_id=1, source_target_pairs={{0,4},{4,0},{8,12},{12,8},{16,20},{20,16},{24,28},{28,24},{1,5},{5... | collective-permute-start | bytes 4718600 | tf_op jit(solution)/shard_map/ppermute | solution.py:933
  484.2 38.3 %collective-permute-start.49 = (f32[192,768]{1,0:T(8,128)}, f32[192,768]{1,0:T(8,128)}, u32[]{:S(2)}, u32[]{:S(2)}) collective-permute-start(f32[192,768]{1,0:T(8,128)} %get-tuple-element.161), channel_id=1, source_target_pairs={{0,16},{4,20},{8,24},{12,28},{16,0},{20,4},{24,8},{28,12},{1,17},{... | collective-permute-start | bytes 1769480 | tf_op jit(solution)/shard_map/ppermute | solution.py:940
  484.2 38.3 %collective-permute-start.50 = (f32[192,768]{1,0:T(8,128)}, f32[192,768]{1,0:T(8,128)}, u32[]{:S(2)}, u32[]{:S(2)}) collective-permute-start(f32[192,768]{1,0:T(8,128)} %get-tuple-element.162), channel_id=1, source_target_pairs={{0,24},{4,28},{8,16},{12,20},{16,8},{20,12},{24,0},{28,4},{1,25},{... | collective-permute-start | bytes 1769480 | tf_op jit(solution)/shard_map/ppermute | solution.py:940
  491.1 113.6 %collective-permute-start.26 = (bf16[512,1536]{1,0:T(8,128)(2,1)}, bf16[512,1536]{1,0:T(8,128)(2,1)}, u32[]{:S(2)}, u32[]{:S(2)}) collective-permute-start(bf16[512,1536]{1,0:T(8,128)(2,1)} %fusion.4.refs_0_), channel_id=1, source_target_pairs={{0,2},{1,3},{2,0},{3,1},{4,6},{5,7},{6,4},{7,5},{8,10},{9,11},{10,... | collective-permute-start | bytes 4718600 | tf_op jit(solution)/shard_map/ppermute | solution.py:1235
  522.5 41.1 %collective-permute-start.52 = (f32[192,768]{1,0:T(8,128)}, f32[192,768]{1,0:T(8,128)}, u32[]{:S(2)}, u32[]{:S(2)}) collective-permute-start(f32[192,768]{1,0:T(8,128)} %get-tuple-element.166), channel_id=1, source_target_pairs={{0,8},{4,12},{8,0},{12,4},{16,24},{20,28},{24,16},{28,20},{1,9},{5... | collective-permute-start | bytes 1769480 | tf_op jit(solution)/shard_map/ppermute | solution.py:940
  522.5 35.0 %collective-permute-start.53 = (bf16[192,768]{1,0:T(8,128)(2,1)}, bf16[192,768]{1,0:T(8,128)(2,1)S(1)}, u32[]{:S(2)}, u32[]{:S(2)}) collective-permute-start(bf16[192,768]{1,0:T(8,128)(2,1)} %get-tuple-element.167), channel_id=1, source_target_pairs={{0,16},{4,20},{8,24},{12,28},{16,0},{20,4},{24,8},{28,12},{1,17},{... | collective-permute-start | bytes 884744 | tf_op jit(solution)/shard_map/ppermute | solution.py:940
  536.8 26.5 %collective-permute-start.54 = (bf16[192,768]{1,0:T(8,128)(2,1)}, bf16[192,768]{1,0:T(8,128)(2,1)}, u32[]{:S(2)}, u32[]{:S(2)}) collective-permute-start(bf16[192,768]{1,0:T(8,128)(2,1)} %get-tuple-element.168), channel_id=1, source_target_pairs={{0,24},{4,28},{8,16},{12,20},{16,8},{20,12},{24,0},{28,4},{1,25},{... | collective-permute-start | bytes 884744 | tf_op jit(solution)/shard_map/ppermute | solution.py:940
  557.6 36.7 %collective-permute-start.33 = (bf16[256,1536]{1,0:T(8,128)(2,1)}, bf16[256,1536]{1,0:T(8,128)(2,1)S(1)}, u32[]{:S(2)}, u32[]{:S(2)}) collective-permute-start(bf16[256,1536]{1,0:T(8,128)(2,1)} %get-tuple-element.140), channel_id=1, source_target_pairs={{0,2},{1,3},{2,0},{3,1},{4,6},{5,7},{6,4},{7,5},{8,10},{9,11},{10,... | collective-permute-start | bytes 2359304 | tf_op jit(solution)/shard_map/ppermute | solution.py:1271
  558.3 40.3 %collective-permute-start.31 = (bf16[256,1536]{1,0:T(8,128)(2,1)}, bf16[256,1536]{1,0:T(8,128)(2,1)S(1)}, u32[]{:S(2)}, u32[]{:S(2)}) collective-permute-start(bf16[256,1536]{1,0:T(8,128)(2,1)} %get-tuple-element.138), channel_id=1, source_target_pairs={{0,2},{1,3},{2,0},{3,1},{4,6},{5,7},{6,4},{7,5},{8,10},{9,11},{10,... | collective-permute-start | bytes 2359304 | tf_op jit(solution)/shard_map/ppermute | solution.py:1271
  563.6 22.4 %collective-permute-start.46 = (bf16[192,512]{1,0:T(8,128)(2,1)}, bf16[192,512]{1,0:T(8,128)(2,1)S(1)}, u32[]{:S(2)}, u32[]{:S(2)}) collective-permute-start(bf16[192,512]{1,0:T(8,128)(2,1)} %get-tuple-element.153), channel_id=1, source_target_pairs={{0,24},{4,28},{8,16},{12,20},{16,8},{20,12},{24,0},{28,4},{1,25},{... | collective-permute-start | bytes 589832 | tf_op jit(solution)/shard_map/ppermute | solution.py:940
  604.3 79.7 %collective-permute-start.25 = (bf16[512,1536]{1,0:T(8,128)(2,1)}, bf16[512,1536]{1,0:T(8,128)(2,1)S(1)}, u32[]{:S(2)}, u32[]{:S(2)}) collective-permute-start(bf16[512,1536]{1,0:T(8,128)(2,1)} %fusion.4.refs_0_), channel_id=1, source_target_pairs={{0,1},{1,0},{2,3},{3,2},{4,5},{5,4},{6,7},{7,6},{8,9},{9,8},{10,11... | collective-permute-start | bytes 4718600 | tf_op jit(solution)/shard_map/ppermute | solution.py:1236
  604.7 79.3 %collective-permute-start.27 = (bf16[512,1536]{1,0:T(8,128)(2,1)}, bf16[512,1536]{1,0:T(8,128)(2,1)S(1)}, u32[]{:S(2)}, u32[]{:S(2)}) collective-permute-start(bf16[512,1536]{1,0:T(8,128)(2,1)} %collective-permute-done.26.refs_2_), channel_id=1, source_target_pairs={{0,1},{1,0},{2,3},{3,2},{4,5},{5,4},{6,7},{7,6},{8,9},{9,8},{10,11... | collective-permute-start | bytes 4718600 | tf_op jit(solution)/shard_map/ppermute | solution.py:1237
  629.2 35.5 %collective-permute-start.69 = (f32[12,64,128]{2,1,0:T(8,128)}, f32[12,64,128]{2,1,0:T(8,128)}, u32[]{:S(2)}, u32[]{:S(2)}) collective-permute-start(f32[12,64,128]{2,1,0:T(8,128)} %add.322.gram_ref), channel_id=1, source_target_pairs={{0,16},{4,20},{8,24},{12,28},{16,0},{20,4},{24,8},{28,12},{1,17},{... | collective-permute-start | bytes 1179656 | tf_op jit(solution)/shard_map/ppermute | solution.py:950
  645.9 31.0 %collective-permute-start.66 = (f32[6,64,128]{2,1,0:T(8,128)S(1)}, f32[6,64,128]{2,1,0:T(8,128)}, u32[]{:S(2)}, u32[]{:S(2)}) collective-permute-start(f32[6,64,128]{2,1,0:T(8,128)S(1)} %add.320.gram_ref), channel_id=1, source_target_pairs={{0,16},{4,20},{8,24},{12,28},{16,0},{20,4},{24,8},{28,12},{1,17},{... | collective-permute-start | bytes 589832 | tf_op jit(solution)/shard_map/ppermute | solution.py:950
  651.2 45.0 %collective-permute-start.63 = (f32[320,128]{1,0:T(8,128)}, f32[320,128]{1,0:T(8,128)}, u32[]{:S(2)}, u32[]{:S(2)}) collective-permute-start(f32[320,128]{1,0:T(8,128)} %add.317), channel_id=1, source_target_pairs={{0,16},{4,20},{8,24},{12,28},{16,0},{20,4},{24,8},{28,12},{1,17},{... | collective-permute-start | bytes 491528 | tf_op jit(solution)/shard_map/ppermute | solution.py:950
  692.4 52.7 %collective-permute-start.38 = (bf16[256,1536]{1,0:T(8,128)(2,1)}, bf16[256,1536]{1,0:T(8,128)(2,1)S(1)}, u32[]{:S(2)}, u32[]{:S(2)}) collective-permute-start(bf16[256,1536]{1,0:T(8,128)(2,1)} %get-tuple-element.141.refs_2_), channel_id=1, source_target_pairs={{0,1},{1,0},{2,3},{3,2},{4,5},{5,4},{6,7},{7,6},{8,9},{9,8},{10,11... | collective-permute-start | bytes 2359304 | tf_op jit(solution)/shard_map/ppermute | solution.py:1278
  693.2 51.8 %collective-permute-start.37 = (bf16[256,1536]{1,0:T(8,128)(2,1)}, bf16[256,1536]{1,0:T(8,128)(2,1)S(1)}, u32[]{:S(2)}, u32[]{:S(2)}) collective-permute-start(bf16[256,1536]{1,0:T(8,128)(2,1)} %get-tuple-element.139.refs_1_), channel_id=1, source_target_pairs={{0,1},{1,0},{2,3},{3,2},{4,5},{5,4},{6,7},{7,6},{8,9},{9,8},{10,11... | collective-permute-start | bytes 2359304 | tf_op jit(solution)/shard_map/ppermute | solution.py:1278
  693.5 35.9 %collective-permute-start.32 = (bf16[256,1536]{1,0:T(8,128)(2,1)}, bf16[256,1536]{1,0:T(8,128)(2,1)S(1)}, u32[]{:S(2)}, u32[]{:S(2)}) collective-permute-start(bf16[256,1536]{1,0:T(8,128)(2,1)} %get-tuple-element.139.refs_1_), channel_id=1, source_target_pairs={{0,2},{1,3},{2,0},{3,1},{4,6},{5,7},{6,4},{7,5},{8,10},{9,11},{10,... | collective-permute-start | bytes 2359304 | tf_op jit(solution)/shard_map/ppermute | solution.py:1276
  713.0 40.8 %collective-permute-start.36 = (bf16[256,1536]{1,0:T(8,128)(2,1)S(1)}, bf16[256,1536]{1,0:T(8,128)(2,1)}, u32[]{:S(2)}, u32[]{:S(2)}) collective-permute-start(bf16[256,1536]{1,0:T(8,128)(2,1)S(1)} %collective-permute-done.34.refs_2_), channel_id=1, source_target_pairs={{0,1},{1,0},{2,3},{3,2},{4,5},{5,4},{6,7},{7,6},{8,9},{9,8},{10,11... | collective-permute-start | bytes 2359304 | tf_op jit(solution)/shard_map/ppermute | solution.py:1280
  729.4 24.5 %collective-permute-start.35 = (bf16[256,1536]{1,0:T(8,128)(2,1)S(1)}, bf16[256,1536]{1,0:T(8,128)(2,1)}, u32[]{:S(2)}, u32[]{:S(2)}) collective-permute-start(bf16[256,1536]{1,0:T(8,128)(2,1)S(1)} %collective-permute-done.32.refs_1_), channel_id=1, source_target_pairs={{0,1},{1,0},{2,3},{3,2},{4,5},{5,4},{6,7},{7,6},{8,9},{9,8},{10,11... | collective-permute-start | bytes 2359304 | tf_op jit(solution)/shard_map/ppermute | solution.py:1280
  (146 other events, 1649.9 us)
